TPU v7x, 512 devices: a whole 4x8x8 slice. The times are simulated.
512 devices in a mesh: tm: 128 (over y, z, core), batch: 4 (over x).
Axes of the slice: x: 4, y: 8, z: 8, core: 2. Of those that a mesh axis runs over, the one named last changes fastest.
Arguments:
- latents: bfloat16 [4, 32768, 512], P('batch', 'tm'), may hold values from -6 to 6
- w_now: bfloat16 [512, 1024], replicated, may hold values from -0.1875 to 0.1875
- w_delay: bfloat16 [512, 1024], replicated, may hold values from -0.1875 to 0.1875
- w_pred: bfloat16 [512, 512], replicated, may hold values from -0.25 to 0.25
- neg_owner: int32 [4, 32768, 4], P('batch', 'tm'), may hold values from 0 to 127, all different within a row; in each aligned block of 256 rows (0 to 255, 256 to 511, ..., all dimensions but the last counted through in order) at most 16 rows name the same one
- neg_block: int32 [4, 32768, 4], P('batch', 'tm'), may hold values from 0 to 1
Outputs:
- grad_delay: float32 [512, 1024], P('tm')
- grad_pred: float32 [512, 512], P('tm')
- frame_loss: float32 [4, 32768], P('batch', 'tm')
Inputs may be any that keep to these rules, and one draw needn't show every extreme that they name: `neg_owner`: A frame's 4 entries are different. Among the 256 frames of one tm index of one recording, no shard is named more than 16 times, and in some such group one shard is named exactly 16 times.
All inputs are finite; a program needn't handle non-finite values.
Results may differ from a plain program's by a relative error of at most 0.011.
Values may be sent and summed in bfloat16 or wider, within the bound.
A program may use at most 64 MiB of HBM per device.

v0:
```python
import jax
import jax.numpy as jnp
from jax import lax
from jax.sharding import PartitionSpec as P

BLOCK = 128
KSTEP = 12
SPAN = 4


rho_radius = 16.0
norm_eps = 1e-06


def from_behind(value, axis, steps):
    count = lax.axis_size(axis)
    leading, last = (max(0, -steps), min(count, count - steps))
    return lax.ppermute(value, axis, [(source, source + steps) for source in range(leading, last)])


def contract_rows(left, right):
    return lax.dot_general(
        left, right, (((0,), (0,)), ((), ())), preferred_element_type=jnp.float32
    )


def slot_places(owners_flat, shards):
    onehot = (owners_flat[:, None] == jnp.arange(shards, dtype=jnp.int32)[None, :]).astype(
        jnp.int32
    )
    rank_table = jnp.cumsum(onehot, axis=0) - 1
    return jnp.sum(rank_table * onehot, axis=1)


def contrast(predicted, target, negatives, valid_mask, loss_weight, inv_root, neg_count):
    positive = (
        jnp.einsum("fc,fc->f", predicted, target, preferred_element_type=jnp.float32) * inv_root
    )
    against = (
        jnp.einsum("fc,fnc->fn", predicted, negatives, preferred_element_type=jnp.float32)
        * inv_root
    )
    scores = jnp.concatenate([positive[:, None], against], 1)
    top_score = jnp.max(scores, axis=1)
    log_total = top_score + jnp.log(jnp.sum(jnp.exp(scores - top_score[:, None]), axis=1))
    probs = jnp.exp(scores - log_total[:, None])
    frame_loss_terms = valid_mask * (log_total - positive)
    first_hot = (jnp.arange(neg_count + 1) == 0).astype(jnp.float32)
    dscores = loss_weight * valid_mask[:, None] * (probs - first_hot[None, :])
    accum = dscores[:, :1] * target.astype(jnp.float32)
    for which in range(neg_count):
        accum = accum + dscores[:, which + 1 : which + 2] * negatives[:, which].astype(jnp.float32)
    return ((accum * inv_root).astype(jnp.bfloat16), frame_loss_terms)


def body(latents, w_now, w_delay, w_pred, neg_owner, neg_block):
    latent_codes = latents[0]
    frames, channels = latent_codes.shape
    shards = lax.axis_size("tm")
    local_shard_index = lax.axis_index("tm")
    half_rows = frames // 2
    neg_count = neg_owner.shape[2]
    capacity = 2 * frames * neg_count // shards
    inv_root = channels ** (-0.5)
    loss_weight = (channels / (lax.axis_size("batch") * (frames * shards - KSTEP))) ** 0.5
    early_half = from_behind(latent_codes[half_rows:], "tm", SPAN + 1)
    late_half = from_behind(latent_codes[:half_rows], "tm", SPAN)
    delayed_latent = jnp.concatenate([early_half, late_half], 0)
    nearby = from_behind(latent_codes[:KSTEP], "tm", -1)
    target = jnp.concatenate([latent_codes[KSTEP:], nearby], 0)
    positions = jnp.arange(frames, dtype=jnp.int32)
    valid_mask = jnp.where(
        (local_shard_index == shards - 1) & (positions >= frames - KSTEP), 0.0, 1.0
    ).astype(jnp.float32)
    owners = neg_owner[0]
    wanted = neg_block[0] * BLOCK + (positions % BLOCK)[:, None]
    owners_flat = owners.reshape(-1)
    wanted_flat = wanted.reshape(-1)
    slot_index = slot_places(owners_flat, shards)
    places = owners_flat * capacity + slot_index
    requests = (
        jnp.zeros((shards * capacity,), jnp.int32)
        .at[places]
        .set(wanted_flat)
        .reshape(shards, capacity)
    )
    picked = latent_codes[lax.all_to_all(requests, "tm", split_axis=0, concat_axis=0, tiled=True)]
    arrived = lax.all_to_all(picked, "tm", split_axis=0, concat_axis=0, tiled=True)
    negatives = arrived.reshape(shards * capacity, channels)[places].reshape(
        frames, neg_count, channels
    )
    pre_now = jnp.dot(latent_codes, w_now, preferred_element_type=jnp.float32)

    def gradient_terms(delay_weight, pred_weight):
        preact = pre_now + jnp.dot(delayed_latent, delay_weight, preferred_element_type=jnp.float32)
        tanh_part = jnp.tanh(preact[:, :channels])
        gate_part = jax.nn.sigmoid(preact[:, channels:])
        context = (latent_codes.astype(jnp.float32) + tanh_part * gate_part).astype(jnp.bfloat16)
        predicted = jnp.dot(context, pred_weight, preferred_element_type=jnp.float32).astype(
            jnp.bfloat16
        )
        pred_grad, frame_loss_terms = contrast(
            predicted, target, negatives, valid_mask, loss_weight, inv_root, neg_count
        )
        context_grad = jnp.dot(pred_grad, pred_weight.T, preferred_element_type=jnp.float32)
        filt_grad = context_grad * (1.0 - tanh_part * tanh_part) * gate_part
        gate_grad = context_grad * tanh_part * gate_part * (1.0 - gate_part)
        preact_grad = jnp.concatenate([filt_grad, gate_grad], 1).astype(jnp.bfloat16)
        return (context, pred_grad, preact_grad, frame_loss_terms)

    context, pred_grad, preact_grad, unused = gradient_terms(w_delay, w_pred)
    term_delay = contract_rows(delayed_latent, preact_grad)
    term_pred = contract_rows(context, pred_grad)
    first_delay, first_pred = lax.psum((term_delay, term_pred), ("tm", "batch"))
    grad_norm = jnp.sqrt(jnp.sum(first_delay * first_delay) + jnp.sum(first_pred * first_pred))
    step_scale = rho_radius / (grad_norm + norm_eps)
    delay_up = (w_delay.astype(jnp.float32) + step_scale * first_delay).astype(jnp.bfloat16)
    pred_up = (w_pred.astype(jnp.float32) + step_scale * first_pred).astype(jnp.bfloat16)
    context_up, pred_grad_up, preact_grad_up, frame_loss_terms = gradient_terms(delay_up, pred_up)
    shard_terms = lax.psum_scatter(
        jnp.concatenate(
            [
                contract_rows(delayed_latent, preact_grad_up),
                contract_rows(context_up, pred_grad_up),
            ],
            1,
        ),
        "tm",
        scatter_dimension=0,
        tiled=True,
    )
    summed = lax.psum(shard_terms, "batch")
    return (summed[:, : 2 * channels], summed[:, 2 * channels :], frame_loss_terms[None, :])


def solution(mesh):
    return jax.shard_map(
        body,
        mesh=mesh,
        in_specs=(
            P("batch", "tm", None),
            P(),
            P(),
            P(),
            P("batch", "tm", None),
            P("batch", "tm", None),
        ),
        out_specs=(P("tm", None), P("tm", None), P("batch", "tm")),
        check_vma=False,
    )
```

profile of v0, /device:TPU:1, one launch (start us, length us, event | category | flops | bytes accessed | tf_op | source)
XLA Modules:
  0.0 670.0 jit_solution(13268948978266365990)
XLA Ops:
  11.3 4.3 scatter_custom_fusion
  15.7 29.7 %all_to_all.17 = s32[128,1,16]{2,1,0:T(1,128)S(1)} all-to-all(s32[128,1,16]{2,1,0:T(1,128)S(1)} %bitcast.104), channel_id=1, replica_groups=mesh['tm'=128,'batch'=4] {'tm'}, dimensions={0} | all-to-all | bytes 16384 | tf_op jit(solution)/shard_map/all_to_all | solution.py:87
  45.6 9.2 %gather_fusion = bf16[2048,512]{1,0:T(8,128)(2,1)} fusion(bf16[256,512]{1,0:T(8,128)(2,1)S(1)} %bitcast.101, s32[2048]{0:T(1024)S(1)} %broadcast_clamp_fusion), kind=kCustom, calls=%fused_computation | custom fusion | bytes 4202496 | tf_op jit(solution)/shard_map/gather | solution.py:87
  54.7 5.8 all-to-all-start.1
  61.3 6.0 collective-permute-start
  67.3 3.7 collective-permute-start.1
  71.6 3.1 collective-permute-start.2
  75.5 1.4 fusion.58
  78.1 29.6 %collective-permute-done = bf16[128,512]{1,0:T(8,128)(2,1)} collective-permute-done((bf16[128,512]{1,0:T(8,128)(2,1)}, bf16[128,512]{1,0:T(8,128)(2,1)}, u32[]{:S(2)}, u32[]{:S(2)}) %collective-permute-start) | collective-permute-done | bytes 131104 | tf_op jit(solution)/shard_map/ppermute | solution.py:18
  108.6 3.7 collective-permute-done.1
  112.3 2.1 convolution_add_fusion.1
  115.6 1.6 fusion.15
  117.1 5.0 gather_fusion.1
  123.5 2.4 fusion.64
  129.9 1.7 fusion.8
  133.9 1.8 fusion.23
  135.7 292.8 %all-reduce.7.cloned.1.call-done = (f32[512,1024]{1,0:T(8,128)}, f32[512,512]{1,0:T(8,128)}) async-done(((f32[512,1024]{1,0:T(8,128)}, f32[512,512]{1,0:T(8,128)}), (f32[512,1024]{1,0:T(8,128)}, f32[512,512]{1,0:T(8,128)})) %all-reduce.7.cloned.1.call-update) | async-done | bytes 3145744 | tf_op jit(solution)/shard_map/psum | solution.py:114
  428.5 2.8 multiply_reduce_fusion
  433.6 1.7 add_convert_fusion.2
  435.7 2.0 convolution_add_fusion
  442.9 1.6 fusion.14
  446.3 1.9 pad_maximum_fusion
  450.2 197.8 %all-reduce.5.cloned.1.call-done = f32[512,1536]{1,0:T(8,128)} async-done(((f32[512,1536]{1,0:T(8,128)}), f32[512,1536]{1,0:T(8,128)}) %all-reduce.5.cloned.1.call-update) | async-done | bytes 3145744
  648.7 13.2 %psum.23 = f32[4,1536]{1,0:T(4,128)S(1)} all-reduce(f32[4,1536]{1,0:T(4,128)S(1)} %constant_dynamic-slice_fusion), channel_id=1, replica_groups=mesh['tm'=128,'batch'=4] {'batch'}, use_global_device_ids=true, to_apply=%region_13.14 | all-reduce | flops 6144 | bytes 49152 | tf_op jit(solution)/shard_map/psum | solution.py:132
  (133 shorter events, 28.4 us)
Async XLA Ops:
  7.2 68.3 %copy-start = (bf16[512,1024]{1,0:T(8,128)(2,1)S(1)}, bf16[512,1024]{1,0:T(8,128)(2,1)}, u32[]{:S(2)}) copy-start(bf16[512,1024]{1,0:T(8,128)(2,1)} %param.7) | copy-start | bytes 3145732
  9.3 36.2 %copy-start.1 = (bf16[1,256,512]{2,1,0:T(8,128)(2,1)S(1)}, bf16[1,256,512]{2,1,0:T(8,128)(2,1)}, u32[]{:S(2)}) copy-start(bf16[1,256,512]{2,1,0:T(8,128)(2,1)} %param.6) | copy-start | bytes 786436
  54.7 62.4 %all-to-all-start.1 = ((bf16[128,16,512]{2,1,0:T(8,128)(2,1)}), bf16[128,16,512]{2,1,0:T(8,128)(2,1)S(1)}, u32[]{:S(2)}, u32[]{:S(2)}) async-start(bf16[128,16,512]{2,1,0:T(8,128)(2,1)} %bitcast.103), calls=%async_computation.1 | async-start | bytes 4194304 | tf_op jit(solution)/shard_map/all_to_all | solution.py:88
  60.5 368.0 %all-reduce.7.cloned.1.call-start = ((), (), s32[]{:S(2)}) async-start(), calls=%async_computation.3 | async-start | bytes 6291456 | tf_op jit(solution)/shard_map/psum | solution.py:114
  60.5 16.3 %copy-start.28 = (s32[1024,1]{0,1:T(1,128)S(1)}, s32[1024,1]{0,1:T(1,128)}, u32[]{:S(2)}) copy-start(s32[1024,1]{0,1:T(1,128)} %copy-done.27) | copy-start | bytes 12292
  61.3 46.4 %collective-permute-start = (bf16[128,512]{1,0:T(8,128)(2,1)}, bf16[128,512]{1,0:T(8,128)(2,1)}, u32[]{:S(2)}, u32[]{:S(2)}) collective-permute-start(bf16[128,512]{1,0:T(8,128)(2,1)} %get-tuple-element.16), channel_id=1, source_target_pairs={{0,20},{4,24},{8,28},{12,32},{16,36},{20,40},{24,44},{28,48},{32,5... | collective-permute-start | bytes 393224 | tf_op jit(solution)/shard_map/ppermute | solution.py:18
  67.3 45.0 %collective-permute-start.1 = (bf16[128,512]{1,0:T(8,128)(2,1)}, bf16[128,512]{1,0:T(8,128)(2,1)S(1)}, u32[]{:S(2)}, u32[]{:S(2)}) collective-permute-start(bf16[128,512]{1,0:T(8,128)(2,1)} %get-tuple-element.15), channel_id=1, source_target_pairs={{0,16},{4,20},{8,24},{12,28},{16,32},{20,36},{24,40},{28,44},{32,4... | collective-permute-start | bytes 393224 | tf_op jit(solution)/shard_map/ppermute | solution.py:18
  71.6 43.1 %collective-permute-start.2 = (bf16[12,512]{1,0:T(8,128)(2,1)}, bf16[12,512]{1,0:T(8,128)(2,1)S(1)}, u32[]{:S(2)}, u32[]{:S(2)}) collective-permute-start(bf16[12,512]{1,0:T(8,128)(2,1)} %slice_bitcast_fusion.3), channel_id=1, source_target_pairs={{4,0},{8,4},{12,8},{16,12},{20,16},{24,20},{28,24},{32,28},{36,32}... | collective-permute-start | bytes 36872 | tf_op jit(solution)/shard_map/ppermute | solution.py:18
  112.3 3.2 copy-start.16
  112.3 3.2 copy-start.22
  114.5 2.7 copy-start.26
  125.9 3.9 copy-start.7
  125.9 3.9 copy-start.9
  127.6 4.0 copy-start.19
  129.1 3.9 copy-start.29
  129.8 3.1 copy-start.13
  129.8 3.1 copy-start.23
  135.7 512.2 %all-reduce.5.cloned.1.call-start = ((), (), s32[]{:S(2)}) async-start(), calls=%async_computation.2 | async-start | bytes 6291456
  428.5 2.8 copy-start.11
  431.4 3.9 copy-start.2
  438.9 3.9 copy-start.8
  438.9 3.9 copy-start.10
  439.9 4.6 copy-start.15
  440.0 4.5 copy-start.25
  (14 other events, 21.8 us)
Sparse Core Ops, SparseCore 0:
  135.8 292.6 all-reduce.6
  448.3 199.5 all-reduce.4
where the time goes:
time: 675 us; the launch traced here: 670 us
  waiting for transfers between devices  524 us (78%)
  blocking collectives  42.9 us (6%)
  local copies, waits for them, and re-layouts  34.3 us (5%)
  starting transfers between devices  18.7 us (3%)
  other arithmetic  18.6 us (3%)
  between operations  16.6 us (2%)
  matrix products  14.9 us (2%)
    psum x1, waiting for transfers between devices, body(): first_delay, first_pred = lax.psum((term_delay, term_pred), ('tm', 'batch'))  293 us
    unnamed x3, waiting for transfers between devices  198 us
    ppermute x3, waiting for transfers between devices, from_behind(): lax.ppermute(value, axis, [(source, source + steps) for source in range(l...  33.3 us
    all_to_all x1, blocking collectives, body(): lax.all_to_all(requests, 'tm', split_axis=0, concat_axis=0, tiled=True)  29.7 us
  transfers between devices with their start and end apart: 6, of which 4 were waited for; matrix products, arithmetic and copies ran while one was open for 2% of the time, Pallas kernels for 0%

commit v1 on v0

v1 whole, which is shorter than its diff:
```python
import jax
import jax.numpy as jnp
from jax import lax
from jax.sharding import PartitionSpec as P

BLOCK = 128
KSTEP = 12
LAG = 9
RHO = 16.0
EPS = 1e-06


def contract_rows(left, right):
    return lax.dot_general(left, right, (((0,), (0,)), ((), ())), preferred_element_type=jnp.float32)


def times_transposed(left, right):
    return lax.dot_general(left, right, (((1,), (1,)), ((), ())), preferred_element_type=jnp.float32)


def down(value, rows):
    return jnp.concatenate([jnp.zeros((rows, value.shape[1]), value.dtype), value[:-rows]], 0)


def up(value):
    return jnp.concatenate([value[1:], jnp.zeros((1, value.shape[1]), value.dtype)], 0)


def body(latents, w_now, w_delay, w_pred, neg_owner, neg_block):
    codes = latents[0]
    frames, channels = codes.shape
    shards = lax.axis_size("tm")
    blocks = frames // BLOCK
    residue = lax.axis_index("tm")
    neg_count = neg_owner.shape[2]
    inv_root = channels ** (-0.5)
    loss_weight = (channels / (lax.axis_size("batch") * (frames * shards - KSTEP))) ** 0.5

    by_residue = jnp.swapaxes(codes.reshape(blocks, BLOCK, channels), 0, 1)
    later = jnp.roll(by_residue, -KSTEP, axis=0)
    names = (neg_owner[0] * blocks + neg_block[0]).astype(jnp.bfloat16)
    names = jnp.swapaxes(names.reshape(blocks, BLOCK, neg_count), 0, 1)
    packed = jnp.concatenate(
        [
            by_residue.reshape(BLOCK, -1),
            later.reshape(BLOCK, -1),
            names.reshape(BLOCK, -1),
            jnp.zeros((BLOCK, BLOCK - blocks * neg_count), jnp.bfloat16),
        ],
        1,
    )
    came = lax.all_to_all(packed, "tm", split_axis=0, concat_axis=0, tiled=True)
    rows = shards * blocks
    wide = blocks * channels
    mine = came[:, :wide].reshape(rows, channels)
    target = came[:, wide : 2 * wide].reshape(rows, channels)
    chosen = came[:, 2 * wide : 2 * wide + blocks * neg_count].reshape(rows, neg_count)
    wraps = residue >= BLOCK - KSTEP
    target = jnp.where(wraps, up(target), target)
    delayed = down(mine, LAG)
    valid = jnp.where(wraps & (jnp.arange(rows) == rows - 1), 0.0, 1.0).astype(jnp.float32)
    hot = chosen.astype(jnp.int32)[:, :, None] == jnp.arange(rows, dtype=jnp.int32)[None, None, :]
    pre_now = jnp.dot(mine, w_now, preferred_element_type=jnp.float32)

    def gradient_terms(delay_weight, pred_weight):
        preact = pre_now + jnp.dot(delayed, delay_weight, preferred_element_type=jnp.float32)
        tanh_part = jnp.tanh(preact[:, :channels])
        gate_part = jax.nn.sigmoid(preact[:, channels:])
        context = (mine.astype(jnp.float32) + tanh_part * gate_part).astype(jnp.bfloat16)
        predicted = jnp.dot(context, pred_weight, preferred_element_type=jnp.float32).astype(jnp.bfloat16)
        positive = jnp.sum(predicted.astype(jnp.float32) * target.astype(jnp.float32), axis=1) * inv_root
        pairs = times_transposed(predicted, mine)
        against = jnp.sum(jnp.where(hot, pairs[:, None, :], 0.0), axis=2) * inv_root
        scores = jnp.concatenate([positive[:, None], against], 1)
        top = jnp.max(scores, axis=1)
        lse = top + jnp.log(jnp.sum(jnp.exp(scores - top[:, None]), axis=1))
        losses = valid * (lse - positive)
        probs = jnp.exp(scores - lse[:, None])
        scale = (loss_weight * valid)[:, None]
        d_pos = scale * (probs[:, :1] - 1.0)
        d_neg = scale * probs[:, 1:]
        spread = jnp.sum(jnp.where(hot, d_neg[:, :, None], 0.0), axis=1)
        high = spread.astype(jnp.bfloat16)
        low = (spread - high.astype(jnp.float32)).astype(jnp.bfloat16)
        pulled = jnp.dot(high, mine, preferred_element_type=jnp.float32) + jnp.dot(
            low, mine, preferred_element_type=jnp.float32
        )
        d_pred = ((d_pos * target.astype(jnp.float32) + pulled) * inv_root).astype(jnp.bfloat16)
        d_context = times_transposed(d_pred, pred_weight)
        d_filt = d_context * (1.0 - tanh_part * tanh_part) * gate_part
        d_gate = d_context * tanh_part * gate_part * (1.0 - gate_part)
        d_preact = jnp.concatenate([d_filt, d_gate], 1).astype(jnp.bfloat16)
        return contract_rows(delayed, d_preact), contract_rows(context, d_pred), losses

    def scattered(part_delay, part_pred):
        part = jnp.concatenate([part_delay, part_pred], 1).astype(jnp.bfloat16)
        pieces = lax.all_to_all(part, "tm", split_axis=0, concat_axis=0, tiled=True)
        pieces = pieces.reshape(shards, channels // shards, part.shape[1]).astype(jnp.float32)
        return lax.psum(jnp.sum(pieces, axis=0), "batch")

    first_delay, first_pred, _ = gradient_terms(w_delay, w_pred)
    mean_up = scattered(first_delay, first_pred)
    first = lax.all_gather(mean_up.astype(jnp.bfloat16), "tm", axis=0, tiled=True).astype(jnp.float32)
    step = RHO / (jnp.sqrt(jnp.sum(first * first)) + EPS)
    delay_up = (w_delay.astype(jnp.float32) + step * first[:, : 2 * channels]).astype(jnp.bfloat16)
    pred_up = (w_pred.astype(jnp.float32) + step * first[:, 2 * channels :]).astype(jnp.bfloat16)
    second_delay, second_pred, losses = gradient_terms(delay_up, pred_up)
    summed = scattered(second_delay, second_pred)
    back = lax.all_to_all(losses.reshape(shards, blocks), "tm", split_axis=0, concat_axis=0, tiled=True)
    frame_loss = jnp.swapaxes(back, 0, 1).reshape(1, frames)
    return summed[:, : 2 * channels], summed[:, 2 * channels :], frame_loss


def solution(mesh):
    return jax.shard_map(
        body,
        mesh=mesh,
        in_specs=(P("batch", "tm", None), P(), P(), P(), P("batch", "tm", None), P("batch", "tm", None)),
        out_specs=(P("tm", None), P("tm", None), P("batch", "tm")),
        check_vma=False,
    )
```

time: 675 us -> 322 us (0.48)
  waiting for transfers between devices: 524 us -> 148 us
  blocking collectives: 42.9 us -> 74.7 us
  local copies, waits for them, and re-layouts: 34.3 us -> 16.4 us
  starting transfers between devices: 18.7 us -> 35.1 us
    psum x1 -> x0, waiting for transfers between devices: 293 us -> none  [body(): first_delay, first_pred = lax.psum((term_delay, term_pred), ('tm', 'batch'))]
    unnamed x3 -> x1, waiting for transfers between devices: 198 us -> 0.02 us
    all_gather x0 -> x1, waiting for transfers between devices: none -> 80.3 us  [body(): lax.all_gather(mean_up.astype(jnp.bfloat16), 'tm', axis=0, tiled=True)]
    all_to_all x1 -> x3, waiting for transfers between devices: 0.01 us -> 67.9 us  [the longest x1 40.5 us: scattered(): pieces = lax.all_to_all(part, 'tm', split_axis=0, concat_axis=0, tiled=True)]
    ppermute x3 -> x0, waiting for transfers between devices: 33.3 us -> none  [from_behind(): lax.ppermute(value, axis, [(source, source + steps) for source in range(l...]
    all_to_all x1 -> x3, starting transfers between devices: 5.76 us -> 35 us  [the longest x1 18.4 us: body(): came = lax.all_to_all(packed, 'tm', split_axis=0, concat_axis=0, tiled=True)]
    all_to_all x1, blocking collectives: 29.7 us -> 47.6 us  [scattered(): pieces = lax.all_to_all(part, 'tm', split_axis=0, concat_axis=0, tiled=True)]
    gather x2 -> x0, local copies, waits for them, and re-layouts: 14.2 us -> none  [the longest x1 9.15 us: body(): latent_codes[lax.all_to_all(requests, 'tm', split_axis=0, concat_axis=0,...]
  transfers between devices with their start and end apart: 6 -> 4, of which waited for: 4 -> 4; matrix products, arithmetic and copies ran while one was open for 2% -> 2% of each run, Pallas kernels for 0% -> 0%
where the time goes in v1:
time: 322 us; the launch traced here: 318 us
  waiting for transfers between devices  148 us (46%)
  blocking collectives  74.7 us (23%)
  starting transfers between devices  35.1 us (11%)
  local copies, waits for them, and re-layouts  16.4 us (5%)
  between operations  15.2 us (5%)
  other arithmetic  15.1 us (5%)
  matrix products  13.3 us (4%)
    all_gather x1, waiting for transfers between devices, body(): lax.all_gather(mean_up.astype(jnp.bfloat16), 'tm', axis=0, tiled=True)  80.3 us
    all_to_all x1, blocking collectives, scattered(): pieces = lax.all_to_all(part, 'tm', split_axis=0, concat_axis=0, tiled=True)  47.6 us
    all_to_all x1, waiting for transfers between devices, scattered(): pieces = lax.all_to_all(part, 'tm', split_axis=0, concat_axis=0, tiled=True)  40.5 us
    psum x2, blocking collectives, scattered(): return lax.psum(jnp.sum(pieces, axis=0), 'batch')  27.1 us
    all_to_all x1, waiting for transfers between devices, body(): came = lax.all_to_all(packed, 'tm', split_axis=0, concat_axis=0, tiled=True)  20.9 us
    all_to_all x1, starting transfers between devices, body(): came = lax.all_to_all(packed, 'tm', split_axis=0, concat_axis=0, tiled=True)  18.4 us
    all_to_all x1, starting transfers between devices, body(): lax.all_to_all(losses.reshape(shards, blocks), 'tm', split_axis=0, concat...  9.48 us
    all_to_all x1, starting transfers between devices, scattered(): pieces = lax.all_to_all(part, 'tm', split_axis=0, concat_axis=0, tiled=True)  7.11 us
  transfers between devices with their start and end apart: 4, of which 4 were waited for; matrix products, arithmetic and copies ran while one was open for 2% of the time, Pallas kernels for 0%

profile of v1, /device:TPU:1, one launch (start us, length us, event | category | flops | bytes accessed | tf_op | source)
XLA Modules:
  0.0 318.0 jit_solution(5047242718851173418)
XLA Ops:
  7.2 1.3 copy.54
  11.8 1.4 reshape.205
  13.1 18.4 %all-to-all-start = ((bf16[128,2,1088]{2,1,0:T(2,128)(2,1)}), bf16[128,2,1088]{2,1,0:T(2,128)(2,1)S(1)}, u32[]{:S(2)}, u32[]{:S(2)}) async-start(bf16[128,2,1088]{2,1,0:T(2,128)(2,1)} %reshape.205), calls=%async_computation | async-start | bytes 1179648 | tf_op jit(solution)/shard_map/all_to_all | solution.py:52
  31.6 20.9 %all-to-all-done = bf16[128,2,1088]{2,1,0:T(2,128)(2,1)S(1)} async-done(((bf16[128,2,1088]{2,1,0:T(2,128)(2,1)}), bf16[128,2,1088]{2,1,0:T(2,128)(2,1)S(1)}, u32[]{:S(2)}, u32[]{:S(2)}) %all-to-all-start) | async-done | bytes 557088 | tf_op jit(solution)/shard_map/all_to_all | solution.py:52
  54.2 1.7 convolution_add_fusion.1
  58.2 1.3 multiply_convert_fusion.3
  60.7 2.5 convolution_convert_fusion.1
  63.3 2.3 concatenate.51
  65.5 1.9 pad_maximum_fusion
  67.5 47.6 %all_to_all.33 = bf16[128,4,1536]{2,1,0:T(4,128)(2,1)S(1)} all-to-all(bf16[128,4,1536]{2,1,0:T(4,128)(2,1)S(1)} %pad_maximum_fusion), channel_id=1, replica_groups=mesh['tm'=128,'batch'=4] {'tm'}, dimensions={0} | all-to-all | bytes 3145728 | tf_op jit(solution)/shard_map/all_to_all | solution.py:97
  115.8 13.9 %psum.14 = bf16[4,1536]{1,0:T(4,128)(2,1)} all-reduce(f32[4,1536]{1,0:T(4,128)S(1)} %convert_reduce_fusion.1), channel_id=1, replica_groups=mesh['tm'=128,'batch'=4] {'batch'}, use_global_device_ids=true, to_apply=%region_6.7 | all-reduce | flops 6144 | bytes 36864 | tf_op jit(solution)/shard_map/psum | solution.py:99
  129.7 80.3 %all-gather.3.cloned.1.call-done = bf16[128,4,1536]{2,1,0:T(4,128)(2,1)} async-done(((bf16[1,4,1536]{2,1,0:T(4,128)(2,1)}), bf16[128,4,1536]{2,1,0:T(4,128)(2,1)}) %all-gather.3.cloned.1.call-update) | async-done | bytes 1572880 | tf_op jit(solution)/shard_map/all_gather | solution.py:103
  210.0 3.9 %reshape.204 = f32[512,1536]{1,0:T(8,128)} reshape(bf16[128,4,1536]{2,1,0:T(4,128)(2,1)} %all-gather.3.cloned.1.call-done) | data formatting | bytes 4718592 | tf_op jit(solution)/shard_map/convert_element_type | solution.py:103
  213.9 3.3 %multiply_reduce_fusion = f32[]{:T(128)} fusion(f32[512,1536]{1,0:T(8,128)} %reshape.204), kind=kLoop, calls=%fused_computation.1 | loop fusion | flops 1572863 | bytes 3145732 | tf_op jit(solution)/shard_map/reduce_sum | solution.py:104
  217.9 2.5 convolution_add_fusion
  220.4 1.8 fusion.10
  226.8 9.5 %all-to-all-start.3 = ((f32[128,1,2]{2,1,0:T(1,128)}), f32[128,1,2]{2,1,0:T(1,128)S(1)}, u32[]{:S(2)}, u32[]{:S(2)}) async-start(f32[128,1,2]{2,1,0:T(1,128)} %bitcast.11), calls=%async_computation.3 | async-start | bytes 131072 | tf_op jit(solution)/shard_map/all_to_all | solution.py:109
  236.4 1.5 convolution_convert_fusion
  237.9 1.5 concatenate.56
  239.3 1.9 pad_maximum_fusion.1
  241.2 6.6 %all-to-all-done.3 = f32[128,1,2]{2,1,0:T(1,128)S(1)} async-done(((f32[128,1,2]{2,1,0:T(1,128)}), f32[128,1,2]{2,1,0:T(1,128)S(1)}, u32[]{:S(2)}, u32[]{:S(2)}) %all-to-all-start.3) | async-done | bytes 1056 | tf_op jit(solution)/shard_map/all_to_all | solution.py:109
  247.8 7.1 %all-to-all-start.2 = ((bf16[128,4,1536]{2,1,0:T(4,128)(2,1)}), bf16[128,4,1536]{2,1,0:T(4,128)(2,1)S(1)}, u32[]{:S(2)}, u32[]{:S(2)}) async-start(bf16[128,4,1536]{2,1,0:T(4,128)(2,1)} %pad_maximum_fusion.1), calls=%async_computation.2 | async-start | bytes 3145728 | tf_op jit(solution)/shard_map/all_to_all | solution.py:97
  255.6 40.5 %all-to-all-done.2 = bf16[128,4,1536]{2,1,0:T(4,128)(2,1)S(1)} async-done(((bf16[128,4,1536]{2,1,0:T(4,128)(2,1)}), bf16[128,4,1536]{2,1,0:T(4,128)(2,1)S(1)}, u32[]{:S(2)}, u32[]{:S(2)}) %all-to-all-start.2) | async-done | bytes 1572896 | tf_op jit(solution)/shard_map/all_to_all | solution.py:97
  296.7 13.2 %psum.15 = f32[4,1536]{1,0:T(4,128)S(1)} all-reduce(f32[4,1536]{1,0:T(4,128)S(1)} %convert_reduce_fusion), channel_id=1, replica_groups=mesh['tm'=128,'batch'=4] {'batch'}, use_global_device_ids=true, to_apply=%region_14.15 | all-reduce | flops 6144 | bytes 49152 | tf_op jit(solution)/shard_map/psum | solution.py:99
  (83 shorter events, 16.1 us)
Async XLA Ops:
  7.2 46.6 %copy-start = (bf16[512,1024]{1,0:T(8,128)(2,1)S(1)}, bf16[512,1024]{1,0:T(8,128)(2,1)}, u32[]{:S(2)}) copy-start(bf16[512,1024]{1,0:T(8,128)(2,1)} %param.7) | copy-start | bytes 3145732
  13.1 39.3 %all-to-all-start = ((bf16[128,2,1088]{2,1,0:T(2,128)(2,1)}), bf16[128,2,1088]{2,1,0:T(2,128)(2,1)S(1)}, u32[]{:S(2)}, u32[]{:S(2)}) async-start(bf16[128,2,1088]{2,1,0:T(2,128)(2,1)} %reshape.205), calls=%async_computation | async-start | bytes 1179648 | tf_op jit(solution)/shard_map/all_to_all | solution.py:52
  31.6 178.4 %all-gather.3.cloned.1.call-start = ((), (), s32[]{:S(2)}) async-start(), calls=%async_computation.4 | async-start | bytes 1585152 | tf_op jit(solution)/shard_map/all_gather | solution.py:103
  54.2 2.0 copy-start.5
  60.7 4.8 %copy-start.7 = (bf16[128,4,512]{2,1,0:T(4,128)(2,1)S(1)}, bf16[128,4,512]{2,1,0:T(4,128)(2,1)}, u32[]{:S(2)}) copy-start(bf16[128,4,512]{2,1,0:T(4,128)(2,1)} %concatenate.52) | copy-start | bytes 1572868
  217.9 2.5 copy-start.6
  220.4 2.5 copy-start.1
  222.2 0.8 copy-start.3
  223.0 1.9 copy-start.2
  224.1 1.1 copy-start.4
  226.8 21.0 %all-to-all-start.3 = ((f32[128,1,2]{2,1,0:T(1,128)}), f32[128,1,2]{2,1,0:T(1,128)S(1)}, u32[]{:S(2)}, u32[]{:S(2)}) async-start(f32[128,1,2]{2,1,0:T(1,128)} %bitcast.11), calls=%async_computation.3 | async-start | bytes 131072 | tf_op jit(solution)/shard_map/all_to_all | solution.py:109
  247.8 48.2 %all-to-all-start.2 = ((bf16[128,4,1536]{2,1,0:T(4,128)(2,1)}), bf16[128,4,1536]{2,1,0:T(4,128)(2,1)S(1)}, u32[]{:S(2)}, u32[]{:S(2)}) async-start(bf16[128,4,1536]{2,1,0:T(4,128)(2,1)} %pad_maximum_fusion.1), calls=%async_computation.2 | async-start | bytes 3145728 | tf_op jit(solution)/shard_map/all_to_all | solution.py:97
Sparse Core Ops, SparseCore 0:
  129.8 80.1 all-gather.2

commit v2 on v1

v2 whole, which is shorter than its diff:
```python
import jax
import jax.numpy as jnp
from jax import lax
from jax.experimental import pallas as pl
from jax.experimental.pallas import tpu as pltpu
from jax.sharding import PartitionSpec as P

BLOCK = 128
KSTEP = 12
LAG = 9
NNEG = 4
RHO = 16.0
EPS = 1e-06
NY = NZ = 8
NX = 4
CH = 512
WIDE = 384
F32 = jnp.float32
BF16 = jnp.bfloat16


def contract_rows(left, right):
    return lax.dot_general(left, right, (((0,), (0,)), ((), ())), preferred_element_type=F32)


def times_transposed(left, right):
    return lax.dot_general(left, right, (((1,), (1,)), ((), ())), preferred_element_type=F32)


def product(left, right):
    return jnp.dot(left, right, preferred_element_type=F32)


def send(src, dst, sems, index, tm, batch):
    copy = pltpu.make_async_remote_copy(
        src_ref=src,
        dst_ref=dst,
        send_sem=sems.at[0, index],
        recv_sem=sems.at[1, index],
        device_id={"tm": tm, "batch": batch},
        device_id_type=pl.DeviceIdType.MESH,
    )
    copy.start()
    return copy


def step_kernel(
    mine_ref,
    target_ref,
    chosen_ref,
    w_now_ref,
    w_delay_ref,
    w_pred_ref,
    grad_delay_ref,
    grad_pred_ref,
    loss_ref,
    delayed_ref,
    pre_now_ref,
    tanh_ref,
    gate_ref,
    context_ref,
    d_pred_ref,
    d_pre_ref,
    delay_up_ref,
    pred_up_ref,
    part_ref,
    core_ref,
    sum_ref,
    wide_ref,
    half_ref,
    thin_ref,
    across_ref,
    whole_ref,
    core_sems,
    wide_sems,
    thin_sems,
    across_sems,
    gather_sems,
    spread_sems,
    pair_sems,
):
    me = lax.axis_index("tm")
    x = lax.axis_index("batch")
    y, z, c = me // (2 * NZ), (me // 2) % NZ, me % 2

    def place(yy, zz, cc):
        return (yy * NZ + zz) * 2 + cc

    others_y = [lax.rem(y + k, NY) for k in range(1, NY)]
    others_z = [lax.rem(z + k, NZ) for k in range(1, NZ)]
    u = x * 2 + c
    others_u = [lax.rem(u + k, 2 * NX) for k in range(1, 2 * NX)]

    barrier = pltpu.get_barrier_semaphore()

    def greet(tm, batch):
        pl.semaphore_signal(
            barrier, inc=1, device_id={"tm": tm, "batch": batch}, device_id_type=pl.DeviceIdType.MESH
        )

    for yy in others_y:
        greet(place(yy, z, c), x)
    for zz in others_z:
        greet(place(y, zz, c), x)
    for uu in others_u:
        greet(place(y, z, uu % 2), uu // 2)

    rows, channels = mine_ref.shape
    inv_root = channels ** (-0.5)
    loss_weight = (channels / (NX * (BLOCK * rows - KSTEP))) ** 0.5
    row_of = lax.broadcasted_iota(jnp.int32, (rows, 1), 0)
    valid = jnp.where((me >= BLOCK - KSTEP) & (row_of == rows - 1), 0.0, 1.0).astype(F32)
    column_of = lax.broadcasted_iota(jnp.int32, (rows, rows), 1)

    shifted = pltpu.roll(mine_ref[...].astype(F32), LAG, 0)
    delayed_ref[...] = jnp.where(row_of >= LAG, shifted, 0.0).astype(BF16)
    pre_now_ref[...] = product(mine_ref[...], w_now_ref[...])

    def gradient(delay_ref, pred_ref, keep_loss, turn):
        filt = pre_now_ref[:, :channels] + product(delayed_ref[...], delay_ref[:, :channels])
        gate = pre_now_ref[:, channels:] + product(delayed_ref[...], delay_ref[:, channels:])
        tanh_part = jnp.tanh(filt)
        gate_part = jax.nn.sigmoid(gate)
        tanh_ref[...] = tanh_part
        gate_ref[...] = gate_part
        context_ref[...] = (mine_ref[...].astype(F32) + tanh_part * gate_part).astype(BF16)
        predicted = product(context_ref[...], pred_ref[...]).astype(BF16)
        goal = target_ref[...].astype(F32)
        positive = jnp.sum(predicted.astype(F32) * goal, axis=1, keepdims=True) * inv_root
        pairs = times_transposed(predicted, mine_ref[...])
        names = chosen_ref[...]
        hot = [column_of == names[:, n : n + 1] for n in range(NNEG)]
        against = [
            jnp.sum(jnp.where(hot[n], pairs, 0.0), axis=1, keepdims=True) * inv_root for n in range(NNEG)
        ]
        top = positive
        for score in against:
            top = jnp.maximum(top, score)
        total = jnp.exp(positive - top)
        for score in against:
            total = total + jnp.exp(score - top)
        lse = top + jnp.log(total)
        if keep_loss:
            loss_ref[...] = valid * (lse - positive)
        scale = loss_weight * valid
        d_pos = scale * (jnp.exp(positive - lse) - 1.0)
        spread = jnp.zeros((rows, rows), F32)
        for n in range(NNEG):
            spread = spread + jnp.where(hot[n], scale * jnp.exp(against[n] - lse), 0.0)
        high = spread.astype(BF16)
        low = (spread - high.astype(F32)).astype(BF16)
        pulled = product(high, mine_ref[...]) + product(low, mine_ref[...])
        d_pred_ref[...] = ((d_pos * goal + pulled) * inv_root).astype(BF16)
        d_context = times_transposed(d_pred_ref[...], pred_ref[...])
        tanh_part = tanh_ref[...]
        gate_part = gate_ref[...]
        d_pre_ref[:, :channels] = (d_context * (1.0 - tanh_part * tanh_part) * gate_part).astype(BF16)
        d_pre_ref[:, channels:] = (d_context * tanh_part * gate_part * (1.0 - gate_part)).astype(BF16)

        def store(h, value, low_col, high_col):
            part_ref[turn, h, :, :, low_col:high_col] = value.astype(BF16).reshape(
                NY * NZ, 8, high_col - low_col
            )

        store(0, contract_rows(delayed_ref[...], d_pre_ref[:, :WIDE]), 0, WIDE)
        store(1, contract_rows(delayed_ref[...], d_pre_ref[:, WIDE : 2 * WIDE]), 0, WIDE)
        store(2, contract_rows(delayed_ref[...], d_pre_ref[:, 2 * WIDE :]), 0, 256)
        store(2, contract_rows(context_ref[...], d_pred_ref[:, :128]), 256, WIDE)
        store(3, contract_rows(context_ref[...], d_pred_ref[:, 128:]), 0, WIDE)

    def reduce(turn):
        mate = place(y, z, 1 - c)
        swaps = [
            send(part_ref.at[turn, 2 * (1 - c) + j], core_ref.at[turn, j], core_sems.at[turn], j, mate, x)
            for j in range(2)
        ]
        wide = []
        for j in range(2):
            swaps[j].wait()
            both = part_ref[turn, 2 * c + j].astype(F32) + core_ref[turn, j].astype(F32)
            sum_ref[turn, j] = both.astype(BF16).reshape(NY, NZ, 8, WIDE)
            for k in range(1, 8):
                if j == 0:
                    there = others_y[k - 1]
                    src, tm = sum_ref.at[turn, j, there], place(there, z, c)
                else:
                    there = others_z[k - 1]
                    src, tm = sum_ref.at[turn, j, :, there], place(y, there, c)
                wide.append(
                    send(src, wide_ref.at[turn, j, k - 1], wide_sems.at[turn, j], k - 1, tm, x)
                )
        thin = []
        for j in range(2):
            own = sum_ref[turn, j, y] if j == 0 else sum_ref[turn, j, :, z]
            total = own.astype(F32)
            for k in range(7):
                wide[7 * j + k].wait()
                total = total + wide_ref[turn, j, k].astype(F32)
            half_ref[turn, j] = total.astype(BF16)
            for k in range(1, 8):
                if j == 0:
                    there = others_z[k - 1]
                    tm = place(y, there, c)
                else:
                    there = others_y[k - 1]
                    tm = place(there, z, c)
                thin.append(
                    send(
                        half_ref.at[turn, j, there],
                        thin_ref.at[turn, j, k - 1],
                        thin_sems.at[turn, j],
                        k - 1,
                        tm,
                        x,
                    )
                )
        for j in range(2):
            total = half_ref[turn, j, z if j == 0 else y].astype(F32)
            for k in range(7):
                thin[7 * j + k].wait()
                total = total + thin_ref[turn, j, k].astype(F32)
            across_ref[turn, u, :, j * WIDE : (j + 1) * WIDE] = total

    def cross(turn):
        copies = [
            send(
                across_ref.at[turn, u],
                across_ref.at[turn, u],
                across_sems.at[turn],
                k,
                place(y, z, uu % 2),
                uu // 2,
            )
            for k, uu in enumerate(others_u)
        ]
        for copy in copies:
            copy.wait()

    gradient(w_delay_ref, w_pred_ref, False, 0)
    pl.semaphore_wait(barrier, 21)
    reduce(0)
    cross(0)

    total = across_ref[0, c]
    for xx in range(1, NX):
        total = total + across_ref[0, 2 * xx + c]
    whole_ref[2 * c, y, z] = total[:, :WIDE].astype(BF16)
    whole_ref[2 * c + 1, y, z] = total[:, WIDE:].astype(BF16)
    first = []
    for j in range(2):
        for k in range(7):
            there = others_z[k] if j == 0 else others_y[k]
            tm = place(y, there, c) if j == 0 else place(there, z, c)
            spot = whole_ref.at[2 * c + j, y, z]
            first.append(send(spot, spot, gather_sems.at[j], k, tm, x))
    second = []
    for j in range(2):
        for k in range(7):
            first[7 * j + k].wait()
        for k in range(7):
            there = others_y[k] if j == 0 else others_z[k]
            tm = place(there, z, c) if j == 0 else place(y, there, c)
            spot = whole_ref.at[2 * c + j, y] if j == 0 else whole_ref.at[2 * c + j, :, z]
            second.append(send(spot, spot, spread_sems.at[j], k, tm, x))
    third = []
    for j in range(2):
        for k in range(7):
            second[7 * j + k].wait()
        spot = whole_ref.at[2 * c + j]
        third.append(send(spot, spot, pair_sems, j, place(y, z, 1 - c), x))
    for copy in third:
        copy.wait()

    squares = jnp.zeros((8, 128), F32)
    for h in range(4):
        piece = whole_ref[h].astype(F32).reshape(channels, WIDE)
        squares = squares + jnp.sum((piece * piece).reshape(channels // 8, 8, 3, 128), axis=(0, 2))
    norm = jnp.sqrt(jnp.sum(squares))
    step = RHO / (norm + EPS)
    for h in range(4):
        piece = whole_ref[h].astype(F32).reshape(channels, WIDE) * step
        low, high = h * WIDE, (h + 1) * WIDE
        cut = min(max(2 * channels, low), high)
        if cut > low:
            delay_up_ref[:, low:cut] = (w_delay_ref[:, low:cut].astype(F32) + piece[:, : cut - low]).astype(BF16)
        if cut < high:
            at, to = cut - 2 * channels, high - 2 * channels
            pred_up_ref[:, at:to] = (w_pred_ref[:, at:to].astype(F32) + piece[:, cut - low :]).astype(BF16)

    gradient(delay_up_ref, pred_up_ref, True, 1)
    reduce(1)
    cross(1)
    for j in range(2):
        total = across_ref[1, j]
        for xx in range(1, NX):
            total = total + across_ref[1, 2 * xx + j]
        kept = jnp.where(c == 0, total[:4], total[4:])
        low, high = j * 2 * WIDE, (j + 1) * 2 * WIDE
        cut = min(high, 2 * channels)
        grad_delay_ref[:, low:cut] = kept[:, : cut - low]
        if cut < high:
            grad_pred_ref[:, cut - 2 * channels : high - 2 * channels] = kept[:, cut - low :]


def body(latents, w_now, w_delay, w_pred, neg_owner, neg_block):
    codes = latents[0]
    frames, channels = codes.shape
    shards = lax.axis_size("tm")
    blocks = frames // BLOCK
    residue = lax.axis_index("tm")
    by_residue = jnp.swapaxes(codes.reshape(blocks, BLOCK, channels), 0, 1)
    later = jnp.roll(by_residue, -KSTEP, axis=0)
    names = (neg_owner[0] * blocks + neg_block[0]).astype(BF16)
    names = jnp.swapaxes(names.reshape(blocks, BLOCK, NNEG), 0, 1)
    packed = jnp.concatenate(
        [
            by_residue.reshape(BLOCK, -1),
            later.reshape(BLOCK, -1),
            names.reshape(BLOCK, -1),
            jnp.zeros((BLOCK, BLOCK - blocks * NNEG), BF16),
        ],
        1,
    )
    came = lax.all_to_all(packed, "tm", split_axis=0, concat_axis=0, tiled=True)
    rows = shards * blocks
    wide = blocks * channels
    mine = came[:, :wide].reshape(rows, channels)
    target = came[:, wide : 2 * wide].reshape(rows, channels)
    chosen = came[:, 2 * wide : 2 * wide + blocks * NNEG].reshape(rows, NNEG).astype(jnp.int32)
    next_target = jnp.concatenate([target[1:], jnp.zeros((1, channels), BF16)], 0)
    target = jnp.where(residue >= BLOCK - KSTEP, next_target, target)

    vmem = pl.BlockSpec(memory_space=pltpu.VMEM)
    dma = pltpu.SemaphoreType.DMA
    grad_delay, grad_pred, losses = pl.pallas_call(
        step_kernel,
        out_shape=(
            jax.ShapeDtypeStruct((4, 2 * channels), F32),
            jax.ShapeDtypeStruct((4, channels), F32),
            jax.ShapeDtypeStruct((rows, 1), F32),
        ),
        in_specs=[vmem] * 6,
        out_specs=(vmem, vmem, vmem),
        scratch_shapes=[
            pltpu.VMEM((rows, channels), BF16),
            pltpu.VMEM((rows, 2 * channels), F32),
            pltpu.VMEM((rows, channels), F32),
            pltpu.VMEM((rows, channels), F32),
            pltpu.VMEM((rows, channels), BF16),
            pltpu.VMEM((rows, channels), BF16),
            pltpu.VMEM((rows, 2 * channels), BF16),
            pltpu.VMEM((channels, 2 * channels), BF16),
            pltpu.VMEM((channels, channels), BF16),
            pltpu.VMEM((2, 4, NY * NZ, 8, WIDE), BF16),
            pltpu.VMEM((2, 2, NY * NZ, 8, WIDE), BF16),
            pltpu.VMEM((2, 2, NY, NZ, 8, WIDE), BF16),
            pltpu.VMEM((2, 2, 7, 8, 8, WIDE), BF16),
            pltpu.VMEM((2, 2, 8, 8, WIDE), BF16),
            pltpu.VMEM((2, 2, 7, 8, WIDE), BF16),
            pltpu.VMEM((2, 2 * NX, 8, 2 * WIDE), F32),
            pltpu.VMEM((4, NY, NZ, 8, WIDE), BF16),
            dma((2, 2, 2)),
            dma((2, 2, 2, 7)),
            dma((2, 2, 2, 7)),
            dma((2, 2, 7)),
            dma((2, 2, 7)),
            dma((2, 2, 7)),
            dma((2, 2)),
        ],
        compiler_params=pltpu.CompilerParams(
            collective_id=0, has_side_effects=True, vmem_limit_bytes=48 * 1024 * 1024
        ),
    )(mine, target, chosen, w_now, w_delay, w_pred)
    back = lax.all_to_all(losses.reshape(shards, blocks), "tm", split_axis=0, concat_axis=0, tiled=True)
    frame_loss = jnp.swapaxes(back, 0, 1).reshape(1, frames)
    return grad_delay, grad_pred, frame_loss


def solution(mesh):
    return jax.shard_map(
        body,
        mesh=mesh,
        in_specs=(P("batch", "tm", None), P(), P(), P(), P("batch", "tm", None), P("batch", "tm", None)),
        out_specs=(P("tm", None), P("tm", None), P("batch", "tm")),
        check_vma=False,
    )
```

time: 322 us -> 151 us (0.47); the launches traced: 318 us -> 151 us
  waiting for transfers between devices: 148 us -> 32.4 us
  Pallas kernels: 0 us -> 78.3 us
  blocking collectives: 74.7 us -> 0 us
  between operations: 15.2 us -> 0.82 us
  matrix products: 13.3 us -> 0 us
  other arithmetic: 15.1 us -> 2.16 us
  starting transfers between devices: 35.1 us -> 27.2 us
  local copies, waits for them, and re-layouts: 16.4 us -> 10.1 us
    all_gather x1 -> x0, waiting for transfers between devices: 80.3 us -> none  [body(): lax.all_gather(mean_up.astype(jnp.bfloat16), 'tm', axis=0, tiled=True)]
    pallas_call x0 -> x1, Pallas kernels: none -> 78.3 us  [body(): pl.pallas_call(step_kernel, out_shape=(jax.ShapeDtypeStruct((4, 2 * chann...]
    all_to_all x1 -> x0, blocking collectives: 47.6 us -> none  [scattered(): pieces = lax.all_to_all(part, 'tm', split_axis=0, concat_axis=0, tiled=True)]
    all_to_all x1 -> x0, waiting for transfers between devices: 40.5 us -> none  [scattered(): pieces = lax.all_to_all(part, 'tm', split_axis=0, concat_axis=0, tiled=True)]
    psum x2 -> x0, blocking collectives: 27.1 us -> none  [scattered(): return lax.psum(jnp.sum(pieces, axis=0), 'batch')]
    dot_general x17 -> x0, matrix products: 13.3 us -> none  [the longest x4 4.65 us: contract_rows(): lax.dot_general(left, right, (((0,), (0,)), ((), ())), preferred_element_...]
    all_to_all x1 -> x0, starting transfers between devices: 7.11 us -> none  [scattered(): pieces = lax.all_to_all(part, 'tm', split_axis=0, concat_axis=0, tiled=True)]
    reduce_sum x9 -> x0, other arithmetic: 6.18 us -> none  [the longest x1 3.3 us: body(): step = RHO / (jnp.sqrt(jnp.sum(first * first)) + EPS)]
  transfers between devices with their start and end apart: 4 -> 2, of which waited for: 4 -> 2; matrix products, arithmetic and copies ran while one was open for 2% -> 0% of each run, Pallas kernels for 0% -> 0%
where the time goes in v2:
time: 151 us
  Pallas kernels  78.3 us (52%)
  waiting for transfers between devices  32.4 us (21%)
  starting transfers between devices  27.2 us (18%)
  local copies, waits for them, and re-layouts  10.1 us (7%)
  other arithmetic  2.16 us (1%)
    pallas_call x1, Pallas kernels, body(): pl.pallas_call(step_kernel, out_shape=(jax.ShapeDtypeStruct((4, 2 * chann...  78.3 us
    all_to_all x1, waiting for transfers between devices, body(): came = lax.all_to_all(packed, 'tm', split_axis=0, concat_axis=0, tiled=True)  20.9 us
    all_to_all x1, starting transfers between devices, body(): came = lax.all_to_all(packed, 'tm', split_axis=0, concat_axis=0, tiled=True)  18.4 us
    all_to_all x1, waiting for transfers between devices, body(): lax.all_to_all(losses.reshape(shards, blocks), 'tm', split_axis=0, concat...  11.5 us
    all_to_all x1, starting transfers between devices, body(): lax.all_to_all(losses.reshape(shards, blocks), 'tm', split_axis=0, concat...  8.82 us
    unnamed x17, local copies, waits for them, and re-layouts  3.41 us
  transfers between devices with their start and end apart: 2, of which 2 were waited for; matrix products, arithmetic and copies ran while one was open for 0% of the time, Pallas kernels for 0%

profile of v2, /device:TPU:1, one launch (start us, length us, event | category | flops | bytes accessed | tf_op | source)
XLA Modules:
  0.0 151.1 jit_solution(11019235823431760322)
XLA Ops:
  0.6 1.2 copy.40
  1.9 0.2 slice.26
  2.1 0.3 pad_maximum_fusion
  2.6 0.1 copy.29
  2.7 0.3 concatenate.11
  3.0 0.5 broadcast.6
  3.5 1.0 reduce.1
  4.5 1.4 reshape.48
  5.9 18.4 %all-to-all-start = ((bf16[128,2,1088]{2,1,0:T(2,128)(2,1)}), bf16[128,2,1088]{2,1,0:T(2,128)(2,1)S(1)}, u32[]{:S(2)}, u32[]{:S(2)}) async-start(bf16[128,2,1088]{2,1,0:T(2,128)(2,1)} %reshape.48), calls=%async_computation | async-start | bytes 1179648 | tf_op jit(solution)/shard_map/all_to_all | solution.py:324
  24.3 20.9 %all-to-all-done = bf16[128,2,1088]{2,1,0:T(2,128)(2,1)S(1)} async-done(((bf16[128,2,1088]{2,1,0:T(2,128)(2,1)}), bf16[128,2,1088]{2,1,0:T(2,128)(2,1)S(1)}, u32[]{:S(2)}, u32[]{:S(2)}) %all-to-all-start) | async-done | bytes 557088 | tf_op jit(solution)/shard_map/all_to_all | solution.py:324
  45.2 0.6 reshape.49
  45.9 0.8 fusion
  46.7 0.6 slice_convert_fusion
  47.3 0.1 reshape.44
  47.5 1.2 reshape.43.mine_ref
  48.7 0.9 reshape.46.chosen_ref
  49.7 78.3 %shard_map.85 = (f32[4,1024]{1,0:T(4,128)S(1)}, f32[4,512]{1,0:T(4,128)S(1)}, f32[256,1]{1,0:T(8,128)S(1)}) custom-call(bf16[256,512]{1,0:T(8,128)(2,1)S(1)} %reshape.43.mine_ref, bf16[256,512]{1,0:T(8,128)(2,1)S(1)} %pad_select_fusion.target_ref, s32[256,4]{1,0:T(8,128)S(1)} %reshape.46.chosen_ref, bf16[512,1024]{1,0:T(8,128)(2,1)S(1)} %copy-done, ...), custom_call_target="tpu_custom_call" | custom-call | tf_op jit(solution)/shard_map/pallas_call | solution.py:335
  128.0 0.1 reduce
  128.2 0.8 all_to_all.19
  128.9 8.8 %all-to-all-start.1 = ((f32[128,1,2]{2,1,0:T(1,128)}), f32[128,1,2]{2,1,0:T(1,128)S(1)}, u32[]{:S(2)}, u32[]{:S(2)}) async-start(f32[128,1,2]{2,1,0:T(1,128)} %bitcast.6), calls=%async_computation.1 | async-start | bytes 131072 | tf_op jit(solution)/shard_map/all_to_all | solution.py:374
  137.7 11.5 %all-to-all-done.1 = f32[128,1,2]{2,1,0:T(1,128)S(1)} async-done(((f32[128,1,2]{2,1,0:T(1,128)}), f32[128,1,2]{2,1,0:T(1,128)S(1)}, u32[]{:S(2)}, u32[]{:S(2)}) %all-to-all-start.1) | async-done | bytes 1056 | tf_op jit(solution)/shard_map/all_to_all | solution.py:374
  149.3 0.6 copy.32
  149.9 0.6 copy.44
  150.5 0.6 copy.45
  (18 shorter events, 0.4 us)
Async XLA Ops:
  1.9 0.7 copy-start.3
  1.9 0.7 copy-start.4
  5.9 39.3 %all-to-all-start = ((bf16[128,2,1088]{2,1,0:T(2,128)(2,1)}), bf16[128,2,1088]{2,1,0:T(2,128)(2,1)S(1)}, u32[]{:S(2)}, u32[]{:S(2)}) async-start(bf16[128,2,1088]{2,1,0:T(2,128)(2,1)} %reshape.48), calls=%async_computation | async-start | bytes 1179648 | tf_op jit(solution)/shard_map/all_to_all | solution.py:324
  46.7 3.0 %copy-start.2 = (bf16[512,512]{1,0:T(8,128)(2,1)S(1)}, bf16[512,512]{1,0:T(8,128)(2,1)}, u32[]{:S(2)}) copy-start(bf16[512,512]{1,0:T(8,128)(2,1)} %w_pred_ref.1) | copy-start | bytes 1572868
  47.3 2.4 %copy-start.1 = (bf16[512,1024]{1,0:T(8,128)(2,1)S(1)}, bf16[512,1024]{1,0:T(8,128)(2,1)}, u32[]{:S(2)}) copy-start(bf16[512,1024]{1,0:T(8,128)(2,1)} %w_delay_ref.1) | copy-start | bytes 3145732
  47.4 2.3 %copy-start = (bf16[512,1024]{1,0:T(8,128)(2,1)S(1)}, bf16[512,1024]{1,0:T(8,128)(2,1)}, u32[]{:S(2)}) copy-start(bf16[512,1024]{1,0:T(8,128)(2,1)} %w_now_ref.1) | copy-start | bytes 3145732
  128.9 20.4 %all-to-all-start.1 = ((f32[128,1,2]{2,1,0:T(1,128)}), f32[128,1,2]{2,1,0:T(1,128)S(1)}, u32[]{:S(2)}, u32[]{:S(2)}) async-start(f32[128,1,2]{2,1,0:T(1,128)} %bitcast.6), calls=%async_computation.1 | async-start | bytes 131072 | tf_op jit(solution)/shard_map/all_to_all | solution.py:374

commit v3 on v2

--- a/solution.py
+++ b/solution.py
@@ -44,16 +44,53 @@
     return copy
 
 
+def residue_of(yy, zz, cc):
+    turn = jnp.where((yy & 1) == 0, zz, 2 * NZ - 1 - zz)
+    return ((yy >> 1) + KSTEP * (2 * turn + cc)) & (BLOCK - 1)
+
+
+def ring_place(row, spot):
+    chip, cc = spot // 2, spot % 2
+    back = chip // NZ
+    zz = jnp.where(back == 0, chip, 2 * NZ - 1 - chip)
+    return ((2 * row + back) * NZ + zz) * 2 + cc
+
+
+def picker(picked, count):
+    return jnp.where(lax.broadcasted_iota(jnp.int32, (count, count), 1) == picked, 1.0, 0.0).astype(BF16)
+
+
 def step_kernel(
+    codes_ref,
+    owner_ref,
+    block_ref,
+    w_now_hbm,
+    w_delay_hbm,
+    w_pred_hbm,
+    grad_delay_ref,
+    grad_pred_ref,
+    frame_loss_ref,
+    w_now_ref,
+    w_delay_ref,
+    w_pred_ref,
     mine_ref,
     target_ref,
     chosen_ref,
-    w_now_ref,
-    w_delay_ref,
-    w_pred_ref,
-    grad_delay_ref,
-    grad_pred_ref,
-    loss_ref,
+    names_ref,
+    out_a1_ref,
+    in_a1_ref,
+    out_a2_ref,
+    in_a2_ref,
+    out_b1_ref,
+    in_b1_ref,
+    out_b2_ref,
+    in_b2_ref,
+    loss_y_ref,
+    loss_y_in_ref,
+    loss_z_ref,
+    loss_z_in_ref,
+    loss_c_ref,
+    loss_c_in_ref,
     delayed_ref,
     pre_now_ref,
     tanh_ref,
@@ -71,6 +108,12 @@
     thin_ref,
     across_ref,
     whole_ref,
+    weight_sems,
+    rows_y_sems,
+    rows_v_sems,
+    ring_sems,
+    loss_sems,
+    loss_core_sems,
     core_sems,
     wide_sems,
     thin_sems,
@@ -90,6 +133,13 @@
     others_z = [lax.rem(z + k, NZ) for k in range(1, NZ)]
     u = x * 2 + c
     others_u = [lax.rem(u + k, 2 * NX) for k in range(1, 2 * NX)]
+    v = z * 2 + c
+    others_v = [lax.rem(v + k, 2 * NZ) for k in range(1, 2 * NZ)]
+    row = y // 2
+    spot = 2 * jnp.where(y % 2 == 0, z, 2 * NZ - 1 - z) + c
+    ring_before = ring_place(row, lax.rem(spot + 4 * NZ - 1, 4 * NZ))
+    ring_after = ring_place(row, lax.rem(spot + 1, 4 * NZ))
+    residue = residue_of(y, z, c)
 
     barrier = pltpu.get_barrier_semaphore()
 
@@ -100,23 +150,87 @@
 
     for yy in others_y:
         greet(place(yy, z, c), x)
-    for zz in others_z:
-        greet(place(y, zz, c), x)
-    for uu in others_u:
-        greet(place(y, z, uu % 2), uu // 2)
-
-    rows, channels = mine_ref.shape
+    for vv in others_v:
+        greet(y * 2 * NZ + vv, x)
+    for k in range(1, NX):
+        for cc in range(2):
+            greet(place(y, z, cc), lax.rem(x + k, NX))
+    greet(ring_before, x)
+    greet(ring_after, x)
+
+    loads = [
+        pltpu.make_async_copy(src, dst, weight_sems.at[i])
+        for i, (src, dst) in enumerate(
+            [(w_now_hbm, w_now_ref), (w_delay_hbm, w_delay_ref), (w_pred_hbm, w_pred_ref)]
+        )
+    ]
+    for load in loads:
+        load.start()
+
+    rows, channels = codes_ref.shape
+    cut_a = WIDE
+    order = lax.broadcasted_iota(jnp.int32, (rows, 1), 0)
+    flag = order & 1
+    from_vy = picker((((order >> 2) & 7) << 5) + (((order >> 1) & 1) << 4) + ((order >> 5) << 1) + flag, rows)
+    from_yv = picker((((order >> 1) & 7) << 5) + ((order >> 5) << 2) + (((order >> 4) & 1) << 1) + flag, rows)
+    to_yv = picker(flag * BLOCK + residue_of(order >> 5, (order >> 2) & 7, (order >> 1) & 1), rows)
+    to_vy = picker(flag * BLOCK + residue_of((order >> 1) & 7, order >> 5, (order >> 4) & 1), rows)
+
+    names_ref[...] = jnp.zeros(names_ref.shape, F32)
+    names_ref[:, :NNEG] = (owner_ref[...] * 2 + block_ref[...]).astype(F32)
+    out_a1_ref[...] = product(to_yv, codes_ref[:, :cut_a]).astype(BF16).reshape(out_a1_ref.shape)
+    out_b1_ref[:, :, :128] = product(to_vy, codes_ref[:, cut_a:]).astype(BF16).reshape(2 * NZ, 2 * NY, 128)
+    out_b1_ref[:, :, 128:] = product(to_vy, names_ref[...].astype(BF16)).astype(BF16).reshape(2 * NZ, 2 * NY, 128)
+    pl.semaphore_wait(barrier, 30)
+
+    def over_y(src_ref, dst_ref, turn):
+        dst_ref[y] = src_ref[y]
+        return [
+            send(src_ref.at[yy], dst_ref.at[y], rows_y_sems.at[turn], k, place(yy, z, c), x)
+            for k, yy in enumerate(others_y)
+        ]
+
+    def over_v(src_ref, dst_ref, turn):
+        dst_ref[v] = src_ref[v]
+        return [
+            send(src_ref.at[vv], dst_ref.at[v], rows_v_sems.at[turn], k, y * 2 * NZ + vv, x)
+            for k, vv in enumerate(others_v)
+        ]
+
+    def finish(copies):
+        for copy in copies:
+            copy.wait()
+
+    going_a = over_y(out_a1_ref, in_a1_ref, 0)
+    going_b = over_v(out_b1_ref, in_b1_ref, 0)
+    finish(going_a)
+    out_a2_ref[...] = product(from_yv, in_a1_ref[...].reshape(rows, cut_a)).astype(BF16).reshape(out_a2_ref.shape)
+    going_a = over_v(out_a2_ref, in_a2_ref, 1)
+    finish(going_b)
+    out_b2_ref[...] = product(from_vy, in_b1_ref[...].reshape(rows, 256)).astype(BF16).reshape(out_b2_ref.shape)
+    going_b = over_y(out_b2_ref, in_b2_ref, 1)
+    finish(going_a)
+    mine_ref[:, :cut_a] = product(from_vy, in_a2_ref[...].reshape(rows, cut_a)).astype(BF16)
+    finish(going_b)
+    mine_ref[:, cut_a:] = in_b2_ref[:, :, :128].reshape(rows, 128)
+    chosen_ref[...] = in_b2_ref[:, :, 128:].reshape(rows, 128).astype(F32).astype(jnp.int32)
+    ahead = send(mine_ref, target_ref, ring_sems, 0, ring_before, x)
+
     inv_root = channels ** (-0.5)
     loss_weight = (channels / (NX * (BLOCK * rows - KSTEP))) ** 0.5
     row_of = lax.broadcasted_iota(jnp.int32, (rows, 1), 0)
-    valid = jnp.where((me >= BLOCK - KSTEP) & (row_of == rows - 1), 0.0, 1.0).astype(F32)
+    wraps = residue >= BLOCK - KSTEP
+    valid = jnp.where(wraps & (row_of == rows - 1), 0.0, 1.0).astype(F32)
     column_of = lax.broadcasted_iota(jnp.int32, (rows, rows), 1)
 
     shifted = pltpu.roll(mine_ref[...].astype(F32), LAG, 0)
     delayed_ref[...] = jnp.where(row_of >= LAG, shifted, 0.0).astype(BF16)
+    for load in loads:
+        load.wait()
     pre_now_ref[...] = product(mine_ref[...], w_now_ref[...])
-
-    def gradient(delay_ref, pred_ref, keep_loss, turn):
+    lane = lax.broadcasted_iota(jnp.int32, (8, 128), 1)
+
+    def gradient(delay_ref, pred_ref, turn):
         filt = pre_now_ref[:, :channels] + product(delayed_ref[...], delay_ref[:, :channels])
         gate = pre_now_ref[:, channels:] + product(delayed_ref[...], delay_ref[:, channels:])
         tanh_part = jnp.tanh(filt)
@@ -125,6 +239,11 @@
         gate_ref[...] = gate_part
         context_ref[...] = (mine_ref[...].astype(F32) + tanh_part * gate_part).astype(BF16)
         predicted = product(context_ref[...], pred_ref[...]).astype(BF16)
+        if turn == 0:
+            ahead.wait()
+            raw = target_ref[...].astype(F32)
+            moved = jnp.where(row_of < rows - 1, pltpu.roll(raw, rows - 1, 0), 0.0)
+            target_ref[...] = jnp.where(wraps, moved, raw).astype(BF16)
         goal = target_ref[...].astype(F32)
         positive = jnp.sum(predicted.astype(F32) * goal, axis=1, keepdims=True) * inv_root
         pairs = times_transposed(predicted, mine_ref[...])
@@ -140,8 +259,13 @@
         for score in against:
             total = total + jnp.exp(score - top)
         lse = top + jnp.log(total)
-        if keep_loss:
-            loss_ref[...] = valid * (lse - positive)
+        if turn == 1:
+            losses = jnp.broadcast_to(valid * (lse - positive), (rows, 128))
+            loss_y_ref[...] = losses.reshape(NY, 32, 128)
+            for k, yy in enumerate(others_y):
+                loss_going.append(
+                    send(loss_y_ref.at[yy], loss_y_in_ref.at[k], loss_sems.at[0], k, place(yy, z, c), x)
+                )
         scale = loss_weight * valid
         d_pos = scale * (jnp.exp(positive - lse) - 1.0)
         spread = jnp.zeros((rows, rows), F32)
@@ -168,7 +292,37 @@
         store(2, contract_rows(context_ref[...], d_pred_ref[:, :128]), 256, WIDE)
         store(3, contract_rows(context_ref[...], d_pred_ref[:, 128:]), 0, WIDE)
 
-    def reduce(turn):
+    loss_going = []
+
+    def loss_to_z():
+        finish(loss_going)
+        own = jnp.broadcast_to(((lane & 7) == y)[:1], (32, 128))
+        held = jnp.where(own, loss_y_ref[y], 0.0)
+        for k in range(7):
+            source = lax.rem(y + 7 - k, NY)
+            came = jnp.broadcast_to(((lane & 7) == source)[:1], (32, 128))
+            held = jnp.where(came, loss_y_in_ref[k], held)
+        loss_z_ref[...] = jnp.zeros(loss_z_ref.shape, F32)
+        for zz in range(NZ):
+            loss_z_ref[zz, :4] = held[4 * zz : 4 * zz + 4]
+        loss_going[:] = [
+            send(loss_z_ref.at[zz], loss_z_in_ref.at[k], loss_sems.at[1], k, place(y, zz, c), x)
+            for k, zz in enumerate(others_z)
+        ]
+
+    def loss_to_core():
+        finish(loss_going)
+        held = jnp.where((lane >> 3) == z, loss_z_ref[z], 0.0)
+        for k in range(7):
+            source = lax.rem(z + 7 - k, NZ)
+            held = jnp.where((lane >> 3) == source, loss_z_in_ref[k], held)
+        loss_c_ref[...] = held
+        loss_going[:] = [send(loss_c_ref, loss_c_in_ref, loss_core_sems, 0, place(y, z, 1 - c), x)]
+
+    def nothing():
+        pass
+
+    def reduce(turn, between=nothing, after=nothing):
         mate = place(y, z, 1 - c)
         swaps = [
             send(part_ref.at[turn, 2 * (1 - c) + j], core_ref.at[turn, j], core_sems.at[turn], j, mate, x)
@@ -189,6 +343,7 @@
                 wide.append(
                     send(src, wide_ref.at[turn, j, k - 1], wide_sems.at[turn, j], k - 1, tm, x)
                 )
+        between()
         thin = []
         for j in range(2):
             own = sum_ref[turn, j, y] if j == 0 else sum_ref[turn, j, :, z]
@@ -214,6 +369,7 @@
                         x,
                     )
                 )
+        after()
         for j in range(2):
             total = half_ref[turn, j, z if j == 0 else y].astype(F32)
             for k in range(7):
@@ -236,8 +392,7 @@
         for copy in copies:
             copy.wait()
 
-    gradient(w_delay_ref, w_pred_ref, False, 0)
-    pl.semaphore_wait(barrier, 21)
+    gradient(w_delay_ref, w_pred_ref, 0)
     reduce(0)
     cross(0)
 
@@ -287,9 +442,10 @@
             at, to = cut - 2 * channels, high - 2 * channels
             pred_up_ref[:, at:to] = (w_pred_ref[:, at:to].astype(F32) + piece[:, cut - low :]).astype(BF16)
 
-    gradient(delay_up_ref, pred_up_ref, True, 1)
-    reduce(1)
+    gradient(delay_up_ref, pred_up_ref, 1)
+    reduce(1, loss_to_z, loss_to_core)
     cross(1)
+    finish(loss_going)
     for j in range(2):
         total = across_ref[1, j]
         for xx in range(1, NX):
@@ -301,47 +457,59 @@
         if cut < high:
             grad_pred_ref[:, cut - 2 * channels : high - 2 * channels] = kept[:, cut - low :]
 
+    seat = lax.broadcasted_iota(jnp.int32, (128, 128), 0)
+    column = lax.broadcasted_iota(jnp.int32, (128, 128), 1)
+    back = jnp.zeros((8, 128), F32)
+    for held_ref, cc in ((loss_c_ref, c), (loss_c_in_ref, 1 - c)):
+        spread = (seat < NY * NZ) & (residue_of(seat & 7, (seat >> 3) & 7, cc) == column)
+        back = back + jnp.dot(
+            held_ref[...],
+            jnp.where(spread, 1.0, 0.0),
+            preferred_element_type=F32,
+            precision=lax.Precision.HIGHEST,
+        )
+    kept = jnp.where(c == 0, back[:2], back[2:4])
+    frame_loss_ref[:, :BLOCK] = kept[:1]
+    frame_loss_ref[:, BLOCK:] = kept[1:2]
+
 
 def body(latents, w_now, w_delay, w_pred, neg_owner, neg_block):
     codes = latents[0]
-    frames, channels = codes.shape
-    shards = lax.axis_size("tm")
-    blocks = frames // BLOCK
-    residue = lax.axis_index("tm")
-    by_residue = jnp.swapaxes(codes.reshape(blocks, BLOCK, channels), 0, 1)
-    later = jnp.roll(by_residue, -KSTEP, axis=0)
-    names = (neg_owner[0] * blocks + neg_block[0]).astype(BF16)
-    names = jnp.swapaxes(names.reshape(blocks, BLOCK, NNEG), 0, 1)
-    packed = jnp.concatenate(
-        [
-            by_residue.reshape(BLOCK, -1),
-            later.reshape(BLOCK, -1),
-            names.reshape(BLOCK, -1),
-            jnp.zeros((BLOCK, BLOCK - blocks * NNEG), BF16),
-        ],
-        1,
-    )
-    came = lax.all_to_all(packed, "tm", split_axis=0, concat_axis=0, tiled=True)
-    rows = shards * blocks
-    wide = blocks * channels
-    mine = came[:, :wide].reshape(rows, channels)
-    target = came[:, wide : 2 * wide].reshape(rows, channels)
-    chosen = came[:, 2 * wide : 2 * wide + blocks * NNEG].reshape(rows, NNEG).astype(jnp.int32)
-    next_target = jnp.concatenate([target[1:], jnp.zeros((1, channels), BF16)], 0)
-    target = jnp.where(residue >= BLOCK - KSTEP, next_target, target)
-
+    rows, channels = codes.shape
     vmem = pl.BlockSpec(memory_space=pltpu.VMEM)
+    anywhere = pl.BlockSpec(memory_space=pl.ANY)
     dma = pltpu.SemaphoreType.DMA
-    grad_delay, grad_pred, losses = pl.pallas_call(
+    return pl.pallas_call(
         step_kernel,
         out_shape=(
             jax.ShapeDtypeStruct((4, 2 * channels), F32),
             jax.ShapeDtypeStruct((4, channels), F32),
-            jax.ShapeDtypeStruct((rows, 1), F32),
+            jax.ShapeDtypeStruct((1, rows), F32),
         ),
-        in_specs=[vmem] * 6,
+        in_specs=[vmem] * 3 + [anywhere] * 3,
         out_specs=(vmem, vmem, vmem),
         scratch_shapes=[
+            pltpu.VMEM((channels, 2 * channels), BF16),
+            pltpu.VMEM((channels, 2 * channels), BF16),
+            pltpu.VMEM((channels, channels), BF16),
+            pltpu.VMEM((rows, channels), BF16),
+            pltpu.VMEM((rows, channels), BF16),
+            pltpu.VMEM((rows, 128), jnp.int32),
+            pltpu.VMEM((rows, 128), F32),
+            pltpu.VMEM((8, 32, WIDE), BF16),
+            pltpu.VMEM((8, 32, WIDE), BF16),
+            pltpu.VMEM((16, 16, WIDE), BF16),
+            pltpu.VMEM((16, 16, WIDE), BF16),
+            pltpu.VMEM((16, 16, 256), BF16),
+            pltpu.VMEM((16, 16, 256), BF16),
+            pltpu.VMEM((8, 32, 256), BF16),
+            pltpu.VMEM((8, 32, 256), BF16),
+            pltpu.VMEM((8, 32, 128), F32),
+            pltpu.VMEM((7, 32, 128), F32),
+            pltpu.VMEM((8, 8, 128), F32),
+            pltpu.VMEM((7, 8, 128), F32),
+            pltpu.VMEM((8, 128), F32),
+            pltpu.VMEM((8, 128), F32),
             pltpu.VMEM((rows, channels), BF16),
             pltpu.VMEM((rows, 2 * channels), F32),
             pltpu.VMEM((rows, channels), F32),
@@ -359,6 +527,12 @@
             pltpu.VMEM((2, 2, 7, 8, WIDE), BF16),
             pltpu.VMEM((2, 2 * NX, 8, 2 * WIDE), F32),
             pltpu.VMEM((4, NY, NZ, 8, WIDE), BF16),
+            dma((3,)),
+            dma((2, 2, 7)),
+            dma((2, 2, 15)),
+            dma((2, 1)),
+            dma((2, 2, 7)),
+            dma((2, 1)),
             dma((2, 2, 2)),
             dma((2, 2, 2, 7)),
             dma((2, 2, 2, 7)),
@@ -370,10 +544,7 @@
         compiler_params=pltpu.CompilerParams(
             collective_id=0, has_side_effects=True, vmem_limit_bytes=48 * 1024 * 1024
         ),
-    )(mine, target, chosen, w_now, w_delay, w_pred)
-    back = lax.all_to_all(losses.reshape(shards, blocks), "tm", split_axis=0, concat_axis=0, tiled=True)
-    frame_loss = jnp.swapaxes(back, 0, 1).reshape(1, frames)
-    return grad_delay, grad_pred, frame_loss
+    )(codes, neg_owner[0], neg_block[0], w_now, w_delay, w_pred)
 
 
 def solution(mesh):

time: 151 us -> 119 us (0.79)
  Pallas kernels: 78.3 us -> 111 us
  waiting for transfers between devices: 32.4 us -> 0 us
  starting transfers between devices: 27.2 us -> 0 us
  local copies, waits for them, and re-layouts: 10.1 us -> 6.93 us
  other arithmetic: 2.16 us -> 0 us
    pallas_call x1, Pallas kernels: 78.3 us -> 111 us  [body(): pl.pallas_call(step_kernel, out_shape=(jax.ShapeDtypeStruct((4, 2 * chann...]
    all_to_all x2 -> x0, waiting for transfers between devices: 32.4 us -> none  [the longest x1 20.9 us: body(): came = lax.all_to_all(packed, 'tm', split_axis=0, concat_axis=0, tiled=True)]
    all_to_all x2 -> x0, starting transfers between devices: 27.2 us -> none  [the longest x1 18.4 us: body(): came = lax.all_to_all(packed, 'tm', split_axis=0, concat_axis=0, tiled=True)]
    unnamed x17 -> x13, local copies, waits for them, and re-layouts: 3.41 us -> 6.93 us
  transfers between devices with their start and end apart: 2 -> 0, of which waited for: 2 -> 0; matrix products, arithmetic and copies ran while one was open for 0% -> 0% of each run, Pallas kernels for 0% -> 0%
where the time goes in v3:
time: 119 us
  Pallas kernels  111 us (93%)
  local copies, waits for them, and re-layouts  6.93 us (6%)
    pallas_call x1, Pallas kernels, body(): pl.pallas_call(step_kernel, out_shape=(jax.ShapeDtypeStruct((4, 2 * chann...  111 us
    unnamed x13, local copies, waits for them, and re-layouts  6.93 us

profile of v3, /device:TPU:1, one launch (start us, length us, event | category | flops | bytes accessed | tf_op | source)
XLA Modules:
  0.0 118.5 jit_solution(12616551091816971055)
XLA Ops:
  0.6 0.0 copy-start.3
  0.6 0.9 copy.9
  1.5 0.8 copy.10
  2.3 0.0 copy-done.3
  2.3 0.0 copy-start
  2.4 1.2 %copy-done = bf16[512,1024]{1,0:T(8,128)(2,1)S(1)} copy-done((bf16[512,1024]{1,0:T(8,128)(2,1)S(1)}, bf16[512,1024]{1,0:T(8,128)(2,1)}, u32[]{:S(2)}) %copy-start) | copy-done | bytes 1048600
  3.6 0.0 copy-start.1
  3.6 1.2 %copy-done.1 = bf16[512,1024]{1,0:T(8,128)(2,1)S(1)} copy-done((bf16[512,1024]{1,0:T(8,128)(2,1)S(1)}, bf16[512,1024]{1,0:T(8,128)(2,1)}, u32[]{:S(2)}) %copy-start.1) | copy-done | bytes 1048600
  4.8 0.0 copy-start.2
  4.8 1.0 copy-done.2
  5.8 110.9 %shard_map.85 = (f32[4,1024]{1,0:T(4,128)S(1)}, f32[4,512]{1,0:T(4,128)S(1)}, f32[1,256]{1,0:T(1,128)S(1)}) custom-call(bf16[256,512]{1,0:T(8,128)(2,1)S(1)} %bitcast.5, s32[256,4]{1,0:T(8,128)S(1)} %bitcast.3, s32[256,4]{1,0:T(8,128)S(1)} %bitcast.4, bf16[512,1024]{1,0:T(8,128)(2,1)S(1)} %copy-done, bf16[512,1024]{1,0:T(8,128)(2,1)S(1)} %copy-done.1, ...), custom_call_target="tpu_custom_call" | custom-call | tf_op jit(solution)/shard_map/pallas_call | solution.py:482
  116.7 0.6 copy.14
  117.3 0.6 copy.15
  117.9 0.6 copy.16
Async XLA Ops:
  0.6 1.7 %copy-start.3 = (bf16[1,256,512]{2,1,0:T(8,128)(2,1)S(1)}, bf16[1,256,512]{2,1,0:T(8,128)(2,1)}, u32[]{:S(2)}) copy-start(bf16[1,256,512]{2,1,0:T(8,128)(2,1)} %param.6) | copy-start | bytes 786436
  2.3 1.2 %copy-start = (bf16[512,1024]{1,0:T(8,128)(2,1)S(1)}, bf16[512,1024]{1,0:T(8,128)(2,1)}, u32[]{:S(2)}) copy-start(bf16[512,1024]{1,0:T(8,128)(2,1)} %w_now_hbm.1) | copy-start | bytes 3145732
  3.6 1.2 %copy-start.1 = (bf16[512,1024]{1,0:T(8,128)(2,1)S(1)}, bf16[512,1024]{1,0:T(8,128)(2,1)}, u32[]{:S(2)}) copy-start(bf16[512,1024]{1,0:T(8,128)(2,1)} %w_delay_hbm.1) | copy-start | bytes 3145732
  4.8 1.0 copy-start.2

commit v4 on v3

--- a/solution.py
+++ b/solution.py
@@ -15,6 +15,9 @@
 NX = 4
 CH = 512
 WIDE = 384
+FAR_FIRST = (4, 3, 5, 2, 6, 1, 7)
+NEAR_FIRST = (1, 7, 2, 6, 3, 5, 4)
+FAR_FIRST_WIDE = (8, 9, 7, 6, 10, 11, 5, 4, 12, 13, 3, 2, 14, 15, 1)
 F32 = jnp.float32
 BF16 = jnp.bfloat16
 
@@ -61,22 +64,24 @@
 
 
 def step_kernel(
-    codes_ref,
-    owner_ref,
-    block_ref,
+    codes_hbm,
+    owner_hbm,
+    block_hbm,
     w_now_hbm,
     w_delay_hbm,
     w_pred_hbm,
     grad_delay_ref,
     grad_pred_ref,
     frame_loss_ref,
+    codes_ref,
+    owner_ref,
+    block_ref,
     w_now_ref,
     w_delay_ref,
     w_pred_ref,
     mine_ref,
     target_ref,
     chosen_ref,
-    names_ref,
     out_a1_ref,
     in_a1_ref,
     out_a2_ref,
@@ -101,6 +106,7 @@
     delay_up_ref,
     pred_up_ref,
     part_ref,
+    own_ref,
     core_ref,
     sum_ref,
     wide_ref,
@@ -148,10 +154,10 @@
             barrier, inc=1, device_id={"tm": tm, "batch": batch}, device_id_type=pl.DeviceIdType.MESH
         )
 
-    for yy in others_y:
-        greet(place(yy, z, c), x)
-    for vv in others_v:
-        greet(y * 2 * NZ + vv, x)
+    for k in FAR_FIRST:
+        greet(place(others_y[k - 1], z, c), x)
+    for k in FAR_FIRST_WIDE:
+        greet(y * 2 * NZ + others_v[k - 1], x)
     for k in range(1, NX):
         for cc in range(2):
             greet(place(y, z, cc), lax.rem(x + k, NX))
@@ -161,13 +167,20 @@
     loads = [
         pltpu.make_async_copy(src, dst, weight_sems.at[i])
         for i, (src, dst) in enumerate(
-            [(w_now_hbm, w_now_ref), (w_delay_hbm, w_delay_ref), (w_pred_hbm, w_pred_ref)]
+            [
+                (codes_hbm, codes_ref),
+                (owner_hbm, owner_ref),
+                (block_hbm, block_ref),
+                (w_now_hbm, w_now_ref),
+                (w_delay_hbm, w_delay_ref),
+                (w_pred_hbm, w_pred_ref),
+            ]
         )
     ]
     for load in loads:
         load.start()
 
-    rows, channels = codes_ref.shape
+    rows, channels = codes_hbm.shape
     cut_a = WIDE
     order = lax.broadcasted_iota(jnp.int32, (rows, 1), 0)
     flag = order & 1
@@ -176,25 +189,41 @@
     to_yv = picker(flag * BLOCK + residue_of(order >> 5, (order >> 2) & 7, (order >> 1) & 1), rows)
     to_vy = picker(flag * BLOCK + residue_of((order >> 1) & 7, order >> 5, (order >> 4) & 1), rows)
 
-    names_ref[...] = jnp.zeros(names_ref.shape, F32)
-    names_ref[:, :NNEG] = (owner_ref[...] * 2 + block_ref[...]).astype(F32)
+    for load in loads[:3]:
+        load.wait()
+    names = (owner_ref[...] * 2 + block_ref[...]).astype(F32)
+    names = jnp.concatenate([names, jnp.zeros((128 - NNEG, rows), F32)], 0).astype(BF16)
     out_a1_ref[...] = product(to_yv, codes_ref[:, :cut_a]).astype(BF16).reshape(out_a1_ref.shape)
     out_b1_ref[:, :, :128] = product(to_vy, codes_ref[:, cut_a:]).astype(BF16).reshape(2 * NZ, 2 * NY, 128)
-    out_b1_ref[:, :, 128:] = product(to_vy, names_ref[...].astype(BF16)).astype(BF16).reshape(2 * NZ, 2 * NY, 128)
+    out_b1_ref[:, :, 128:] = times_transposed(to_vy, names).astype(BF16).reshape(2 * NZ, 2 * NY, 128)
     pl.semaphore_wait(barrier, 30)
 
     def over_y(src_ref, dst_ref, turn):
         dst_ref[y] = src_ref[y]
         return [
-            send(src_ref.at[yy], dst_ref.at[y], rows_y_sems.at[turn], k, place(yy, z, c), x)
-            for k, yy in enumerate(others_y)
+            send(
+                src_ref.at[others_y[k - 1]],
+                dst_ref.at[y],
+                rows_y_sems.at[turn],
+                k - 1,
+                place(others_y[k - 1], z, c),
+                x,
+            )
+            for k in FAR_FIRST
         ]
 
     def over_v(src_ref, dst_ref, turn):
         dst_ref[v] = src_ref[v]
         return [
-            send(src_ref.at[vv], dst_ref.at[v], rows_v_sems.at[turn], k, y * 2 * NZ + vv, x)
-            for k, vv in enumerate(others_v)
+            send(
+                src_ref.at[others_v[k - 1]],
+                dst_ref.at[v],
+                rows_v_sems.at[turn],
+                k - 1,
+                y * 2 * NZ + others_v[k - 1],
+                x,
+            )
+            for k in FAR_FIRST_WIDE
         ]
 
     def finish(copies):
@@ -211,10 +240,11 @@
     going_b = over_y(out_b2_ref, in_b2_ref, 1)
     finish(going_a)
     mine_ref[:, :cut_a] = product(from_vy, in_a2_ref[...].reshape(rows, cut_a)).astype(BF16)
+    ahead = [send(mine_ref.at[:, :cut_a], target_ref.at[:, :cut_a], ring_sems, 0, ring_before, x)]
     finish(going_b)
     mine_ref[:, cut_a:] = in_b2_ref[:, :, :128].reshape(rows, 128)
     chosen_ref[...] = in_b2_ref[:, :, 128:].reshape(rows, 128).astype(F32).astype(jnp.int32)
-    ahead = send(mine_ref, target_ref, ring_sems, 0, ring_before, x)
+    ahead.append(send(mine_ref.at[:, cut_a:], target_ref.at[:, cut_a:], ring_sems, 1, ring_before, x))
 
     inv_root = channels ** (-0.5)
     loss_weight = (channels / (NX * (BLOCK * rows - KSTEP))) ** 0.5
@@ -225,7 +255,7 @@
 
     shifted = pltpu.roll(mine_ref[...].astype(F32), LAG, 0)
     delayed_ref[...] = jnp.where(row_of >= LAG, shifted, 0.0).astype(BF16)
-    for load in loads:
+    for load in loads[3:]:
         load.wait()
     pre_now_ref[...] = product(mine_ref[...], w_now_ref[...])
     lane = lax.broadcasted_iota(jnp.int32, (8, 128), 1)
@@ -239,19 +269,19 @@
         gate_ref[...] = gate_part
         context_ref[...] = (mine_ref[...].astype(F32) + tanh_part * gate_part).astype(BF16)
         predicted = product(context_ref[...], pred_ref[...]).astype(BF16)
-        if turn == 0:
-            ahead.wait()
-            raw = target_ref[...].astype(F32)
-            moved = jnp.where(row_of < rows - 1, pltpu.roll(raw, rows - 1, 0), 0.0)
-            target_ref[...] = jnp.where(wraps, moved, raw).astype(BF16)
-        goal = target_ref[...].astype(F32)
-        positive = jnp.sum(predicted.astype(F32) * goal, axis=1, keepdims=True) * inv_root
         pairs = times_transposed(predicted, mine_ref[...])
         names = chosen_ref[...]
         hot = [column_of == names[:, n : n + 1] for n in range(NNEG)]
         against = [
             jnp.sum(jnp.where(hot[n], pairs, 0.0), axis=1, keepdims=True) * inv_root for n in range(NNEG)
         ]
+        if turn == 0:
+            finish(ahead)
+            raw = target_ref[...].astype(F32)
+            moved = jnp.where(row_of < rows - 1, pltpu.roll(raw, rows - 1, 0), 0.0)
+            target_ref[...] = jnp.where(wraps, moved, raw).astype(BF16)
+        goal = target_ref[...].astype(F32)
+        positive = jnp.sum(predicted.astype(F32) * goal, axis=1, keepdims=True) * inv_root
         top = positive
         for score in against:
             top = jnp.maximum(top, score)
@@ -281,17 +311,52 @@
         d_pre_ref[:, :channels] = (d_context * (1.0 - tanh_part * tanh_part) * gate_part).astype(BF16)
         d_pre_ref[:, channels:] = (d_context * tanh_part * gate_part * (1.0 - gate_part)).astype(BF16)
 
-        def store(h, value, low_col, high_col):
-            part_ref[turn, h, :, :, low_col:high_col] = value.astype(BF16).reshape(
-                NY * NZ, 8, high_col - low_col
+        def fill(h, put):
+            low, high = h * WIDE, (h + 1) * WIDE
+            cut = min(max(2 * channels, low), high)
+            if cut > low:
+                put(0, cut - low, contract_rows(delayed_ref[...], d_pre_ref[:, low:cut]))
+            if cut < high:
+                at, to = cut - 2 * channels, high - 2 * channels
+                put(cut - low, WIDE, contract_rows(context_ref[...], d_pred_ref[:, at:to]))
+
+        for j in range(2):
+            for cc in range(2):
+
+                @pl.when(c == cc)
+                def _(j=j, cc=cc):
+                    def put(low, high, value):
+                        part_ref[turn, j, :, :, low:high] = value.astype(BF16).reshape(NY * NZ, 8, high - low)
+
+                    fill(2 * (1 - cc) + j, put)
+
+            swaps.append(
+                send(part_ref.at[turn, j], core_ref.at[turn, j], core_sems.at[turn], j, place(y, z, 1 - c), x)
             )
-
-        store(0, contract_rows(delayed_ref[...], d_pre_ref[:, :WIDE]), 0, WIDE)
-        store(1, contract_rows(delayed_ref[...], d_pre_ref[:, WIDE : 2 * WIDE]), 0, WIDE)
-        store(2, contract_rows(delayed_ref[...], d_pre_ref[:, 2 * WIDE :]), 0, 256)
-        store(2, contract_rows(context_ref[...], d_pred_ref[:, :128]), 256, WIDE)
-        store(3, contract_rows(context_ref[...], d_pred_ref[:, 128:]), 0, WIDE)
-
+        for j in range(2):
+            for cc in range(2):
+
+                @pl.when(c == cc)
+                def _(j=j, cc=cc):
+                    def put(low, high, value):
+                        own_ref[j, :, low:high] = value
+
+                    fill(2 * cc + j, put)
+
+            swaps[2 * turn + j].wait()
+            both = own_ref[j].reshape(NY * NZ, 8, WIDE) + core_ref[turn, j].astype(F32)
+            sum_ref[turn, j] = both.astype(BF16).reshape(NY, NZ, 8, WIDE)
+            for k in FAR_FIRST:
+                if j == 0:
+                    there = others_y[k - 1]
+                    src, tm = sum_ref.at[turn, j, there], place(there, z, c)
+                else:
+                    there = others_z[k - 1]
+                    src, tm = sum_ref.at[turn, j, :, there], place(y, there, c)
+                wide[turn, j, k] = send(src, wide_ref.at[turn, j, k - 1], wide_sems.at[turn, j], k - 1, tm, x)
+
+    swaps = []
+    wide = {}
     loss_going = []
 
     def loss_to_z():
@@ -323,108 +388,102 @@
         pass
 
     def reduce(turn, between=nothing, after=nothing):
-        mate = place(y, z, 1 - c)
-        swaps = [
-            send(part_ref.at[turn, 2 * (1 - c) + j], core_ref.at[turn, j], core_sems.at[turn], j, mate, x)
-            for j in range(2)
-        ]
-        wide = []
-        for j in range(2):
-            swaps[j].wait()
-            both = part_ref[turn, 2 * c + j].astype(F32) + core_ref[turn, j].astype(F32)
-            sum_ref[turn, j] = both.astype(BF16).reshape(NY, NZ, 8, WIDE)
-            for k in range(1, 8):
-                if j == 0:
-                    there = others_y[k - 1]
-                    src, tm = sum_ref.at[turn, j, there], place(there, z, c)
-                else:
-                    there = others_z[k - 1]
-                    src, tm = sum_ref.at[turn, j, :, there], place(y, there, c)
-                wide.append(
-                    send(src, wide_ref.at[turn, j, k - 1], wide_sems.at[turn, j], k - 1, tm, x)
-                )
         between()
-        thin = []
+        thin = {}
         for j in range(2):
             own = sum_ref[turn, j, y] if j == 0 else sum_ref[turn, j, :, z]
             total = own.astype(F32)
-            for k in range(7):
-                wide[7 * j + k].wait()
-                total = total + wide_ref[turn, j, k].astype(F32)
+            for k in NEAR_FIRST:
+                wide[turn, j, k].wait()
+                total = total + wide_ref[turn, j, k - 1].astype(F32)
             half_ref[turn, j] = total.astype(BF16)
-            for k in range(1, 8):
-                if j == 0:
-                    there = others_z[k - 1]
-                    tm = place(y, there, c)
-                else:
-                    there = others_y[k - 1]
-                    tm = place(there, z, c)
-                thin.append(
-                    send(
-                        half_ref.at[turn, j, there],
-                        thin_ref.at[turn, j, k - 1],
-                        thin_sems.at[turn, j],
-                        k - 1,
-                        tm,
-                        x,
-                    )
+            for k in FAR_FIRST:
+                there = others_z[k - 1] if j == 0 else others_y[k - 1]
+                tm = place(y, there, c) if j == 0 else place(there, z, c)
+                thin[j, k] = send(
+                    half_ref.at[turn, j, there],
+                    thin_ref.at[turn, j, k - 1],
+                    thin_sems.at[turn, j],
+                    k - 1,
+                    tm,
+                    x,
                 )
         after()
         for j in range(2):
             total = half_ref[turn, j, z if j == 0 else y].astype(F32)
-            for k in range(7):
-                thin[7 * j + k].wait()
-                total = total + thin_ref[turn, j, k].astype(F32)
+            for k in NEAR_FIRST:
+                thin[j, k].wait()
+                total = total + thin_ref[turn, j, k - 1].astype(F32)
             across_ref[turn, u, :, j * WIDE : (j + 1) * WIDE] = total
 
-    def cross(turn):
-        copies = [
-            send(
-                across_ref.at[turn, u],
-                across_ref.at[turn, u],
-                across_sems.at[turn],
-                k,
-                place(y, z, uu % 2),
-                uu // 2,
-            )
-            for k, uu in enumerate(others_u)
+    def cross(turn, peers):
+        return [
+            send(across_ref.at[turn, u], across_ref.at[turn, u], across_sems.at[turn], k, place(y, z, cc), xx)
+            for k, (cc, xx) in enumerate(peers)
         ]
-        for copy in copies:
-            copy.wait()
 
     gradient(w_delay_ref, w_pred_ref, 0)
     reduce(0)
-    cross(0)
+    finish(cross(0, [(c, lax.rem(x + k, NX)) for k in (2, 1, 3)]))
 
     total = across_ref[0, c]
     for xx in range(1, NX):
         total = total + across_ref[0, 2 * xx + c]
     whole_ref[2 * c, y, z] = total[:, :WIDE].astype(BF16)
     whole_ref[2 * c + 1, y, z] = total[:, WIDE:].astype(BF16)
-    first = []
-    for j in range(2):
-        for k in range(7):
-            there = others_z[k] if j == 0 else others_y[k]
+    first = {}
+    for k in FAR_FIRST:
+        for j in range(2):
+            there = others_z[k - 1] if j == 0 else others_y[k - 1]
             tm = place(y, there, c) if j == 0 else place(there, z, c)
             spot = whole_ref.at[2 * c + j, y, z]
-            first.append(send(spot, spot, gather_sems.at[j], k, tm, x))
-    second = []
+            first[j, k] = send(spot, spot, gather_sems.at[j], k - 1, tm, x)
+
+    def spot_of(j, hop, half=None):
+        along = lax.rem((y if j == 0 else z) + NY + hop, NY)
+        rest = slice(None) if half is None else pl.ds(4 * half, 4)
+        return whole_ref.at[2 * c, along, rest] if j == 0 else whole_ref.at[2 * c + 1, rest, along]
+
+    def pass_on(j, hop, away, index, half=None):
+        to = lax.rem((y if j == 0 else z) + NY + away, NY)
+        tm = place(to, z, c) if j == 0 else place(y, to, c)
+        spot = spot_of(j, hop, half)
+        return send(spot, spot, spread_sems.at[j], index, tm, x)
+
+    def to_mate(j, hop, index):
+        spot = spot_of(j, hop)
+        third.append(send(spot, spot, pair_sems.at[j], index, place(y, z, 1 - c), x))
+
+    third = []
+    second = {}
     for j in range(2):
-        for k in range(7):
-            first[7 * j + k].wait()
-        for k in range(7):
-            there = others_y[k] if j == 0 else others_z[k]
-            tm = place(there, z, c) if j == 0 else place(y, there, c)
-            spot = whole_ref.at[2 * c + j, y] if j == 0 else whole_ref.at[2 * c + j, :, z]
-            second.append(send(spot, spot, spread_sems.at[j], k, tm, x))
-    third = []
+        for k in NEAR_FIRST:
+            first[j, k].wait()
+        for index, away in enumerate((2, -2, 1, -1)):
+            second[j, index] = pass_on(j, 0, away, index)
+        to_mate(j, 0, 0)
     for j in range(2):
-        for k in range(7):
-            second[7 * j + k].wait()
-        spot = whole_ref.at[2 * c + j]
-        third.append(send(spot, spot, pair_sems, j, place(y, z, 1 - c), x))
-    for copy in third:
-        copy.wait()
+        second[j, 0].wait()
+        second[j, 4] = pass_on(j, -2, 2, 4, 0)
+        second[j, 5] = pass_on(j, -2, 1, 5)
+        second[j, 1].wait()
+        second[j, 6] = pass_on(j, 2, -2, 6, 1)
+        second[j, 7] = pass_on(j, 2, -1, 7)
+        second[j, 2].wait()
+        to_mate(j, -1, 1)
+        second[j, 3].wait()
+        to_mate(j, 1, 2)
+        to_mate(j, -2, 3)
+        to_mate(j, 2, 4)
+    for j in range(2):
+        second[j, 5].wait()
+        to_mate(j, -3, 5)
+        second[j, 7].wait()
+        to_mate(j, 3, 6)
+        second[j, 4].wait()
+        second[j, 6].wait()
+        to_mate(j, 4, 7)
+    finish(third)
 
     squares = jnp.zeros((8, 128), F32)
     for h in range(4):
@@ -444,19 +503,8 @@
 
     gradient(delay_up_ref, pred_up_ref, 1)
     reduce(1, loss_to_z, loss_to_core)
-    cross(1)
+    crossing = cross(1, [(uu % 2, uu // 2) for uu in others_u])
     finish(loss_going)
-    for j in range(2):
-        total = across_ref[1, j]
-        for xx in range(1, NX):
-            total = total + across_ref[1, 2 * xx + j]
-        kept = jnp.where(c == 0, total[:4], total[4:])
-        low, high = j * 2 * WIDE, (j + 1) * 2 * WIDE
-        cut = min(high, 2 * channels)
-        grad_delay_ref[:, low:cut] = kept[:, : cut - low]
-        if cut < high:
-            grad_pred_ref[:, cut - 2 * channels : high - 2 * channels] = kept[:, cut - low :]
-
     seat = lax.broadcasted_iota(jnp.int32, (128, 128), 0)
     column = lax.broadcasted_iota(jnp.int32, (128, 128), 1)
     back = jnp.zeros((8, 128), F32)
@@ -471,13 +519,24 @@
     kept = jnp.where(c == 0, back[:2], back[2:4])
     frame_loss_ref[:, :BLOCK] = kept[:1]
     frame_loss_ref[:, BLOCK:] = kept[1:2]
+    finish(crossing)
+    for j in range(2):
+        total = across_ref[1, j]
+        for xx in range(1, NX):
+            total = total + across_ref[1, 2 * xx + j]
+        kept = jnp.where(c == 0, total[:4], total[4:])
+        low, high = j * 2 * WIDE, (j + 1) * 2 * WIDE
+        cut = min(high, 2 * channels)
+        grad_delay_ref[:, low:cut] = kept[:, : cut - low]
+        if cut < high:
+            grad_pred_ref[:, cut - 2 * channels : high - 2 * channels] = kept[:, cut - low :]
 
 
 def body(latents, w_now, w_delay, w_pred, neg_owner, neg_block):
     codes = latents[0]
     rows, channels = codes.shape
     vmem = pl.BlockSpec(memory_space=pltpu.VMEM)
-    anywhere = pl.BlockSpec(memory_space=pl.ANY)
+    stay = pl.BlockSpec(memory_space=pltpu.HBM)
     dma = pltpu.SemaphoreType.DMA
     return pl.pallas_call(
         step_kernel,
@@ -486,16 +545,18 @@
             jax.ShapeDtypeStruct((4, channels), F32),
             jax.ShapeDtypeStruct((1, rows), F32),
         ),
-        in_specs=[vmem] * 3 + [anywhere] * 3,
+        in_specs=[stay] * 6,
         out_specs=(vmem, vmem, vmem),
         scratch_shapes=[
+            pltpu.VMEM((rows, channels), BF16),
+            pltpu.VMEM((NNEG, rows), jnp.int32),
+            pltpu.VMEM((NNEG, rows), jnp.int32),
             pltpu.VMEM((channels, 2 * channels), BF16),
             pltpu.VMEM((channels, 2 * channels), BF16),
             pltpu.VMEM((channels, channels), BF16),
             pltpu.VMEM((rows, channels), BF16),
             pltpu.VMEM((rows, channels), BF16),
             pltpu.VMEM((rows, 128), jnp.int32),
-            pltpu.VMEM((rows, 128), F32),
             pltpu.VMEM((8, 32, WIDE), BF16),
             pltpu.VMEM((8, 32, WIDE), BF16),
             pltpu.VMEM((16, 16, WIDE), BF16),
@@ -519,7 +580,8 @@
             pltpu.VMEM((rows, 2 * channels), BF16),
             pltpu.VMEM((channels, 2 * channels), BF16),
             pltpu.VMEM((channels, channels), BF16),
-            pltpu.VMEM((2, 4, NY * NZ, 8, WIDE), BF16),
+            pltpu.VMEM((2, 2, NY * NZ, 8, WIDE), BF16),
+            pltpu.VMEM((2, channels, WIDE), F32),
             pltpu.VMEM((2, 2, NY * NZ, 8, WIDE), BF16),
             pltpu.VMEM((2, 2, NY, NZ, 8, WIDE), BF16),
             pltpu.VMEM((2, 2, 7, 8, 8, WIDE), BF16),
@@ -527,10 +589,10 @@
             pltpu.VMEM((2, 2, 7, 8, WIDE), BF16),
             pltpu.VMEM((2, 2 * NX, 8, 2 * WIDE), F32),
             pltpu.VMEM((4, NY, NZ, 8, WIDE), BF16),
-            dma((3,)),
+            dma((6,)),
             dma((2, 2, 7)),
             dma((2, 2, 15)),
-            dma((2, 1)),
+            dma((2, 2)),
             dma((2, 2, 7)),
             dma((2, 1)),
             dma((2, 2, 2)),
@@ -538,13 +600,13 @@
             dma((2, 2, 2, 7)),
             dma((2, 2, 7)),
             dma((2, 2, 7)),
-            dma((2, 2, 7)),
-            dma((2, 2)),
+            dma((2, 2, 8)),
+            dma((2, 2, 8)),
         ],
         compiler_params=pltpu.CompilerParams(
-            collective_id=0, has_side_effects=True, vmem_limit_bytes=48 * 1024 * 1024
+            collective_id=0, has_side_effects=True, vmem_limit_bytes=60 * 1024 * 1024
         ),
-    )(codes, neg_owner[0], neg_block[0], w_now, w_delay, w_pred)
+    )(codes, jnp.swapaxes(neg_owner[0], 0, 1), jnp.swapaxes(neg_block[0], 0, 1), w_now, w_delay, w_pred)
 
 
 def solution(mesh):

time: 119 us -> 106 us (0.89)
  Pallas kernels: 111 us -> 102 us
  local copies, waits for them, and re-layouts: 6.93 us -> 2.53 us
    pallas_call x1, Pallas kernels: 111 us -> 102 us  [body(): pl.pallas_call(step_kernel, out_shape=(jax.ShapeDtypeStruct((4, 2 * chann...]
    unnamed x13 -> x7, local copies, waits for them, and re-layouts: 6.93 us -> 2.53 us
where the time goes in v4:
time: 106 us
  Pallas kernels  102 us (96%)
  local copies, waits for them, and re-layouts  2.53 us (2%)
    pallas_call x1, Pallas kernels, body(): pl.pallas_call(step_kernel, out_shape=(jax.ShapeDtypeStruct((4, 2 * chann...  102 us
    unnamed x7, local copies, waits for them, and re-layouts  2.53 us

profile of v4, /device:TPU:1, one launch (start us, length us, event | category | flops | bytes accessed | tf_op | source)
XLA Modules:
  0.0 105.6 jit_solution(13696384629796583702)
XLA Ops:
  0.6 102.5 %shard_map.85 = (f32[4,1024]{1,0:T(4,128)}, f32[4,512]{1,0:T(4,128)}, f32[1,256]{1,0:T(1,128)}) custom-call(bf16[256,512]{1,0:T(8,128)(2,1)} %bitcast.7, s32[4,256]{1,0:T(4,128)} %bitcast.8, s32[4,256]{1,0:T(4,128)} %bitcast.9, bf16[512,1024]{1,0:T(8,128)(2,1)} %w_now_hbm.1, bf16[512,1024]{1,0:T(8,128)(2,1)} %w_delay_hbm.1, bf16[512,512]{1,0:T(8,128)(2,1)} %w_pred_hbm.1), custom_call_target="tpu_custom_call" | custom-call | tf_op jit(solution)/shard_map/pallas_call | solution.py:541
  103.1 0.0 copy-start
  103.1 1.3 %copy.12 = f32[4,1024]{1,0:T(4,128)} copy(f32[4,1024]{1,0:T(4,128)} %get-tuple-element.6) | data formatting | bytes 32768
  104.4 0.0 copy-done
  104.4 0.0 copy-start.1
  104.4 0.6 copy.13
  105.0 0.0 copy-done.1
  105.1 0.6 copy.14
Async XLA Ops:
  103.1 1.3 %copy-start = (f32[4,512]{1,0:T(4,128)S(1)}, f32[4,512]{1,0:T(4,128)}, u32[]{:S(2)}) copy-start(f32[4,512]{1,0:T(4,128)} %get-tuple-element.7) | copy-start | bytes 24580
  104.4 0.6 copy-start.1

commit v5 on v4

--- a/solution.py
+++ b/solution.py
@@ -59,8 +59,8 @@
     return ((2 * row + back) * NZ + zz) * 2 + cc
 
 
-def picker(picked, count):
-    return jnp.where(lax.broadcasted_iota(jnp.int32, (count, count), 1) == picked, 1.0, 0.0).astype(BF16)
+def picker(wanted, count):
+    return jnp.where(lax.broadcasted_iota(jnp.int32, (count, count), 0) == wanted, 1.0, 0.0).astype(BF16)
 
 
 def step_kernel(
@@ -106,7 +106,6 @@
     delay_up_ref,
     pred_up_ref,
     part_ref,
-    own_ref,
     core_ref,
     sum_ref,
     wide_ref,
@@ -124,9 +123,9 @@
     wide_sems,
     thin_sems,
     across_sems,
-    gather_sems,
-    spread_sems,
-    pair_sems,
+    first_sems,
+    second_sems,
+    third_sems,
 ):
     me = lax.axis_index("tm")
     x = lax.axis_index("batch")
@@ -182,12 +181,17 @@
 
     rows, channels = codes_hbm.shape
     cut_a = WIDE
-    order = lax.broadcasted_iota(jnp.int32, (rows, 1), 0)
+    order = lax.broadcasted_iota(jnp.int32, (1, rows), 1)
     flag = order & 1
-    from_vy = picker((((order >> 2) & 7) << 5) + (((order >> 1) & 1) << 4) + ((order >> 5) << 1) + flag, rows)
-    from_yv = picker((((order >> 1) & 7) << 5) + ((order >> 5) << 2) + (((order >> 4) & 1) << 1) + flag, rows)
-    to_yv = picker(flag * BLOCK + residue_of(order >> 5, (order >> 2) & 7, (order >> 1) & 1), rows)
-    to_vy = picker(flag * BLOCK + residue_of((order >> 1) & 7, order >> 5, (order >> 4) & 1), rows)
+    from_vy = picker((((order >> 1) & 7) << 5) + ((order >> 5) << 2) + (((order >> 4) & 1) << 1) + flag, rows)
+    from_yv = picker((((order >> 2) & 7) << 5) + (((order >> 1) & 1) << 4) + ((order >> 5) << 1) + flag, rows)
+    seat = (11 * ((order & (BLOCK - 1)) >> 2)) & 31
+    chip, side, half = seat >> 1, seat & 1, order >> 7
+    back = chip >> 3
+    goal_y = 2 * (order & 3) + back
+    goal_z = jnp.where(back == 0, chip, 2 * NZ - 1 - chip)
+    to_yv = picker((goal_y << 5) + (goal_z << 2) + (side << 1) + half, rows)
+    to_vy = picker((goal_z << 5) + (side << 4) + (goal_y << 1) + half, rows)
 
     for load in loads[:3]:
         load.wait()
@@ -305,58 +309,145 @@
         low = (spread - high.astype(F32)).astype(BF16)
         pulled = product(high, mine_ref[...]) + product(low, mine_ref[...])
         d_pred_ref[...] = ((d_pos * goal + pulled) * inv_root).astype(BF16)
+        swap(turn, 0)
+        mine_first = own_part(0)
         d_context = times_transposed(d_pred_ref[...], pred_ref[...])
         tanh_part = tanh_ref[...]
         gate_part = gate_ref[...]
         d_pre_ref[:, :channels] = (d_context * (1.0 - tanh_part * tanh_part) * gate_part).astype(BF16)
         d_pre_ref[:, channels:] = (d_context * tanh_part * gate_part * (1.0 - gate_part)).astype(BF16)
-
-        def fill(h, put):
-            low, high = h * WIDE, (h + 1) * WIDE
-            cut = min(max(2 * channels, low), high)
-            if cut > low:
-                put(0, cut - low, contract_rows(delayed_ref[...], d_pre_ref[:, low:cut]))
-            if cut < high:
-                at, to = cut - 2 * channels, high - 2 * channels
-                put(cut - low, WIDE, contract_rows(context_ref[...], d_pred_ref[:, at:to]))
-
+        swap(turn, 1)
+        swap(turn, 2)
+        start_wide(turn, 0, mine_first)
+        for t in (1, 2):
+            start_wide(turn, t, own_part(t))
+
+    def own_part(t, cc=c):
+        if t == 0:
+            cols = pl.ds(pl.multiple_of(256 * cc, 256), 256)
+            return contract_rows(context_ref[...], d_pred_ref[:, cols])
+        cols = pl.ds(pl.multiple_of(512 * cc + 256 * (t - 1), 256), 256)
+        return contract_rows(delayed_ref[...], d_pre_ref[:, cols])
+
+    mate = place(y, z, 1 - c)
+    swaps = {}
+    wide = {}
+    thin = {}
+    crossing = {}
+
+    def swap(turn, t):
+        value = own_part(t, 1 - c).astype(BF16).reshape(NY * NZ, 8, 256)
         for j in range(2):
-            for cc in range(2):
-
-                @pl.when(c == cc)
-                def _(j=j, cc=cc):
-                    def put(low, high, value):
-                        part_ref[turn, j, :, :, low:high] = value.astype(BF16).reshape(NY * NZ, 8, high - low)
-
-                    fill(2 * (1 - cc) + j, put)
-
-            swaps.append(
-                send(part_ref.at[turn, j], core_ref.at[turn, j], core_sems.at[turn], j, place(y, z, 1 - c), x)
-            )
+            part_ref[turn, t, j] = value[:, :, 128 * j : 128 * (j + 1)]
+        swaps[turn, t] = send(part_ref.at[turn, t], core_ref.at[turn, t], core_sems.at[turn], t, mate, x)
+
+    def start_wide(turn, t, value):
+        swaps[turn, t].wait()
+        value = value.reshape(NY * NZ, 8, 256)
         for j in range(2):
-            for cc in range(2):
-
-                @pl.when(c == cc)
-                def _(j=j, cc=cc):
-                    def put(low, high, value):
-                        own_ref[j, :, low:high] = value
-
-                    fill(2 * cc + j, put)
-
-            swaps[2 * turn + j].wait()
-            both = own_ref[j].reshape(NY * NZ, 8, WIDE) + core_ref[turn, j].astype(F32)
-            sum_ref[turn, j] = both.astype(BF16).reshape(NY, NZ, 8, WIDE)
+            both = value[:, :, 128 * j : 128 * (j + 1)] + core_ref[turn, t, j].astype(F32)
+            sum_ref[turn, t, j] = both.astype(BF16).reshape(NY, NZ, 8, 128)
             for k in FAR_FIRST:
                 if j == 0:
                     there = others_y[k - 1]
-                    src, tm = sum_ref.at[turn, j, there], place(there, z, c)
+                    src, tm = sum_ref.at[turn, t, j, there], place(there, z, c)
                 else:
                     there = others_z[k - 1]
-                    src, tm = sum_ref.at[turn, j, :, there], place(y, there, c)
-                wide[turn, j, k] = send(src, wide_ref.at[turn, j, k - 1], wide_sems.at[turn, j], k - 1, tm, x)
-
-    swaps = []
-    wide = {}
+                    src, tm = sum_ref.at[turn, t, j, :, there], place(y, there, c)
+                wide[turn, t, j, k] = send(
+                    src, wide_ref.at[turn, t, j, k - 1], wide_sems.at[turn, t, j], k - 1, tm, x
+                )
+
+    def settle_wide(turn, t):
+        for j in range(2):
+            own = sum_ref[turn, t, j, y] if j == 0 else sum_ref[turn, t, j, :, z]
+            total = own.astype(F32)
+            for k in NEAR_FIRST:
+                wide[turn, t, j, k].wait()
+                total = total + wide_ref[turn, t, j, k - 1].astype(F32)
+            half_ref[turn, t, j] = total.astype(BF16)
+            for k in FAR_FIRST:
+                there = others_z[k - 1] if j == 0 else others_y[k - 1]
+                tm = place(y, there, c) if j == 0 else place(there, z, c)
+                thin[turn, t, j, k] = send(
+                    half_ref.at[turn, t, j, there],
+                    thin_ref.at[turn, t, j, k - 1],
+                    thin_sems.at[turn, t, j],
+                    k - 1,
+                    tm,
+                    x,
+                )
+
+    def settle_thin(turn, t):
+        for j in range(2):
+            total = half_ref[turn, t, j, z if j == 0 else y].astype(F32)
+            for k in NEAR_FIRST:
+                thin[turn, t, j, k].wait()
+                total = total + thin_ref[turn, t, j, k - 1].astype(F32)
+            across_ref[turn, t, u, :, 128 * j : 128 * (j + 1)] = total
+        if turn == 0:
+            peers = [(c, lax.rem(x + k, NX)) for k in (2, 1, 3)]
+        else:
+            peers = [(uu % 2, uu // 2) for uu in others_u]
+        spot = across_ref.at[turn, t, u]
+        crossing[turn, t] = [
+            send(spot, spot, across_sems.at[turn, t], k, place(y, z, cc), xx) for k, (cc, xx) in enumerate(peers)
+        ]
+
+    def summed(turn, t, cc):
+        finish(crossing[turn, t])
+        crossing[turn, t] = []
+        total = across_ref[turn, t, cc]
+        for xx in range(1, NX):
+            total = total + across_ref[turn, t, 2 * xx + cc]
+        return total
+
+    first = {}
+    second = {}
+    third = {}
+
+    def settle_cross(t):
+        total = summed(0, t, c).astype(BF16)
+        for j in range(2):
+            whole_ref[c, t, j, y, z] = total[:, 128 * j : 128 * (j + 1)]
+        for k in FAR_FIRST:
+            for j in range(2):
+                there = others_z[k - 1] if j == 0 else others_y[k - 1]
+                tm = place(y, there, c) if j == 0 else place(there, z, c)
+                spot = whole_ref.at[c, t, j, y, z]
+                first[t, j, k] = send(spot, spot, first_sems.at[t, j], k - 1, tm, x)
+
+    def stripe(t, j, along):
+        return whole_ref.at[c, t, j, along] if j == 0 else whole_ref.at[c, t, j, :, along]
+
+    def settle_first(t):
+        for j in range(2):
+            for k in NEAR_FIRST:
+                first[t, j, k].wait()
+            for k in FAR_FIRST:
+                there = others_y[k - 1] if j == 0 else others_z[k - 1]
+                tm = place(there, z, c) if j == 0 else place(y, there, c)
+                spot = stripe(t, j, y if j == 0 else z)
+                second[t, j, k] = send(spot, spot, second_sems.at[t, j], k - 1, tm, x)
+
+    def settle_second(t):
+        third[t] = []
+        if t < 2:
+            for k in NEAR_FIRST:
+                for j in range(2):
+                    second[t, j, k].wait()
+            spot = whole_ref.at[c, t]
+            third[t].append(send(spot, spot, third_sems.at[t, 0], 0, mate, x))
+            return
+        for j in range(2):
+            spot = stripe(t, j, y if j == 0 else z)
+            third[t].append(send(spot, spot, third_sems.at[t, j], 0, mate, x))
+        for k in NEAR_FIRST:
+            for j in range(2):
+                second[t, j, k].wait()
+                spot = stripe(t, j, lax.rem((y if j == 0 else z) + 8 - k, 8))
+                third[t].append(send(spot, spot, third_sems.at[t, j], k, mate, x))
+
     loss_going = []
 
     def loss_to_z():
@@ -384,126 +475,50 @@
         loss_c_ref[...] = held
         loss_going[:] = [send(loss_c_ref, loss_c_in_ref, loss_core_sems, 0, place(y, z, 1 - c), x)]
 
-    def nothing():
-        pass
-
-    def reduce(turn, between=nothing, after=nothing):
-        between()
-        thin = {}
-        for j in range(2):
-            own = sum_ref[turn, j, y] if j == 0 else sum_ref[turn, j, :, z]
-            total = own.astype(F32)
-            for k in NEAR_FIRST:
-                wide[turn, j, k].wait()
-                total = total + wide_ref[turn, j, k - 1].astype(F32)
-            half_ref[turn, j] = total.astype(BF16)
-            for k in FAR_FIRST:
-                there = others_z[k - 1] if j == 0 else others_y[k - 1]
-                tm = place(y, there, c) if j == 0 else place(there, z, c)
-                thin[j, k] = send(
-                    half_ref.at[turn, j, there],
-                    thin_ref.at[turn, j, k - 1],
-                    thin_sems.at[turn, j],
-                    k - 1,
-                    tm,
-                    x,
-                )
-        after()
-        for j in range(2):
-            total = half_ref[turn, j, z if j == 0 else y].astype(F32)
-            for k in NEAR_FIRST:
-                thin[j, k].wait()
-                total = total + thin_ref[turn, j, k - 1].astype(F32)
-            across_ref[turn, u, :, j * WIDE : (j + 1) * WIDE] = total
-
-    def cross(turn, peers):
-        return [
-            send(across_ref.at[turn, u], across_ref.at[turn, u], across_sems.at[turn], k, place(y, z, cc), xx)
-            for k, (cc, xx) in enumerate(peers)
-        ]
-
     gradient(w_delay_ref, w_pred_ref, 0)
-    reduce(0)
-    finish(cross(0, [(c, lax.rem(x + k, NX)) for k in (2, 1, 3)]))
-
-    total = across_ref[0, c]
-    for xx in range(1, NX):
-        total = total + across_ref[0, 2 * xx + c]
-    whole_ref[2 * c, y, z] = total[:, :WIDE].astype(BF16)
-    whole_ref[2 * c + 1, y, z] = total[:, WIDE:].astype(BF16)
-    first = {}
-    for k in FAR_FIRST:
-        for j in range(2):
-            there = others_z[k - 1] if j == 0 else others_y[k - 1]
-            tm = place(y, there, c) if j == 0 else place(there, z, c)
-            spot = whole_ref.at[2 * c + j, y, z]
-            first[j, k] = send(spot, spot, gather_sems.at[j], k - 1, tm, x)
-
-    def spot_of(j, hop, half=None):
-        along = lax.rem((y if j == 0 else z) + NY + hop, NY)
-        rest = slice(None) if half is None else pl.ds(4 * half, 4)
-        return whole_ref.at[2 * c, along, rest] if j == 0 else whole_ref.at[2 * c + 1, rest, along]
-
-    def pass_on(j, hop, away, index, half=None):
-        to = lax.rem((y if j == 0 else z) + NY + away, NY)
-        tm = place(to, z, c) if j == 0 else place(y, to, c)
-        spot = spot_of(j, hop, half)
-        return send(spot, spot, spread_sems.at[j], index, tm, x)
-
-    def to_mate(j, hop, index):
-        spot = spot_of(j, hop)
-        third.append(send(spot, spot, pair_sems.at[j], index, place(y, z, 1 - c), x))
-
-    third = []
-    second = {}
-    for j in range(2):
-        for k in NEAR_FIRST:
-            first[j, k].wait()
-        for index, away in enumerate((2, -2, 1, -1)):
-            second[j, index] = pass_on(j, 0, away, index)
-        to_mate(j, 0, 0)
-    for j in range(2):
-        second[j, 0].wait()
-        second[j, 4] = pass_on(j, -2, 2, 4, 0)
-        second[j, 5] = pass_on(j, -2, 1, 5)
-        second[j, 1].wait()
-        second[j, 6] = pass_on(j, 2, -2, 6, 1)
-        second[j, 7] = pass_on(j, 2, -1, 7)
-        second[j, 2].wait()
-        to_mate(j, -1, 1)
-        second[j, 3].wait()
-        to_mate(j, 1, 2)
-        to_mate(j, -2, 3)
-        to_mate(j, 2, 4)
-    for j in range(2):
-        second[j, 5].wait()
-        to_mate(j, -3, 5)
-        second[j, 7].wait()
-        to_mate(j, 3, 6)
-        second[j, 4].wait()
-        second[j, 6].wait()
-        to_mate(j, 4, 7)
-    finish(third)
+    settle_wide(0, 0)
+    settle_wide(0, 1)
+    settle_wide(0, 2)
+    settle_thin(0, 0)
+    settle_thin(0, 1)
+    settle_cross(0)
+    settle_thin(0, 2)
+    settle_cross(1)
+    settle_first(0)
+    settle_cross(2)
+    settle_first(1)
+    settle_second(0)
+    settle_first(2)
+    settle_second(1)
 
     squares = jnp.zeros((8, 128), F32)
-    for h in range(4):
-        piece = whole_ref[h].astype(F32).reshape(channels, WIDE)
-        squares = squares + jnp.sum((piece * piece).reshape(channels // 8, 8, 3, 128), axis=(0, 2))
+    for t in range(3):
+        if t == 2:
+            settle_second(2)
+        finish(third[t])
+        for cc in range(2):
+            for j in range(2):
+                piece = whole_ref[cc, t, j].astype(F32).reshape(NY * NZ, 8, 128)
+                squares = squares + jnp.sum(piece * piece, axis=0)
     norm = jnp.sqrt(jnp.sum(squares))
     step = RHO / (norm + EPS)
-    for h in range(4):
-        piece = whole_ref[h].astype(F32).reshape(channels, WIDE) * step
-        low, high = h * WIDE, (h + 1) * WIDE
-        cut = min(max(2 * channels, low), high)
-        if cut > low:
-            delay_up_ref[:, low:cut] = (w_delay_ref[:, low:cut].astype(F32) + piece[:, : cut - low]).astype(BF16)
-        if cut < high:
-            at, to = cut - 2 * channels, high - 2 * channels
-            pred_up_ref[:, at:to] = (w_pred_ref[:, at:to].astype(F32) + piece[:, cut - low :]).astype(BF16)
+    for t in range(3):
+        for cc in range(2):
+            for j in range(2):
+                piece = whole_ref[cc, t, j].astype(F32).reshape(channels, 128) * step
+                low = 256 * cc + 128 * j if t == 0 else 512 * cc + 256 * (t - 1) + 128 * j
+                old_ref, new_ref = (w_pred_ref, pred_up_ref) if t == 0 else (w_delay_ref, delay_up_ref)
+                new_ref[:, low : low + 128] = (old_ref[:, low : low + 128].astype(F32) + piece).astype(BF16)
 
     gradient(delay_up_ref, pred_up_ref, 1)
-    reduce(1, loss_to_z, loss_to_core)
-    crossing = cross(1, [(uu % 2, uu // 2) for uu in others_u])
+    settle_wide(1, 0)
+    settle_wide(1, 1)
+    loss_to_z()
+    settle_wide(1, 2)
+    settle_thin(1, 0)
+    settle_thin(1, 1)
+    loss_to_core()
+    settle_thin(1, 2)
     finish(loss_going)
     seat = lax.broadcasted_iota(jnp.int32, (128, 128), 0)
     column = lax.broadcasted_iota(jnp.int32, (128, 128), 1)
@@ -519,17 +534,15 @@
     kept = jnp.where(c == 0, back[:2], back[2:4])
     frame_loss_ref[:, :BLOCK] = kept[:1]
     frame_loss_ref[:, BLOCK:] = kept[1:2]
-    finish(crossing)
-    for j in range(2):
-        total = across_ref[1, j]
-        for xx in range(1, NX):
-            total = total + across_ref[1, 2 * xx + j]
-        kept = jnp.where(c == 0, total[:4], total[4:])
-        low, high = j * 2 * WIDE, (j + 1) * 2 * WIDE
-        cut = min(high, 2 * channels)
-        grad_delay_ref[:, low:cut] = kept[:, : cut - low]
-        if cut < high:
-            grad_pred_ref[:, cut - 2 * channels : high - 2 * channels] = kept[:, cut - low :]
+    for t in range(3):
+        for cc in range(2):
+            total = summed(1, t, cc)
+            kept = jnp.where(c == 0, total[:4], total[4:])
+            if t == 0:
+                grad_pred_ref[:, 256 * cc : 256 * (cc + 1)] = kept
+            else:
+                low = 512 * cc + 256 * (t - 1)
+                grad_delay_ref[:, low : low + 256] = kept
 
 
 def body(latents, w_now, w_delay, w_pred, neg_owner, neg_block):
@@ -580,28 +593,27 @@
             pltpu.VMEM((rows, 2 * channels), BF16),
             pltpu.VMEM((channels, 2 * channels), BF16),
             pltpu.VMEM((channels, channels), BF16),
-            pltpu.VMEM((2, 2, NY * NZ, 8, WIDE), BF16),
-            pltpu.VMEM((2, channels, WIDE), F32),
-            pltpu.VMEM((2, 2, NY * NZ, 8, WIDE), BF16),
-            pltpu.VMEM((2, 2, NY, NZ, 8, WIDE), BF16),
-            pltpu.VMEM((2, 2, 7, 8, 8, WIDE), BF16),
-            pltpu.VMEM((2, 2, 8, 8, WIDE), BF16),
-            pltpu.VMEM((2, 2, 7, 8, WIDE), BF16),
-            pltpu.VMEM((2, 2 * NX, 8, 2 * WIDE), F32),
-            pltpu.VMEM((4, NY, NZ, 8, WIDE), BF16),
+            pltpu.VMEM((2, 3, 2, NY * NZ, 8, 128), BF16),
+            pltpu.VMEM((2, 3, 2, NY * NZ, 8, 128), BF16),
+            pltpu.VMEM((2, 3, 2, NY, NZ, 8, 128), BF16),
+            pltpu.VMEM((2, 3, 2, 7, 8, 8, 128), BF16),
+            pltpu.VMEM((2, 3, 2, 8, 8, 128), BF16),
+            pltpu.VMEM((2, 3, 2, 7, 8, 128), BF16),
+            pltpu.VMEM((2, 3, 2 * NX, 8, 256), F32),
+            pltpu.VMEM((2, 3, 2, NY, NZ, 8, 128), BF16),
             dma((6,)),
             dma((2, 2, 7)),
             dma((2, 2, 15)),
             dma((2, 2)),
             dma((2, 2, 7)),
             dma((2, 1)),
-            dma((2, 2, 2)),
-            dma((2, 2, 2, 7)),
-            dma((2, 2, 2, 7)),
-            dma((2, 2, 7)),
-            dma((2, 2, 7)),
-            dma((2, 2, 8)),
-            dma((2, 2, 8)),
+            dma((2, 2, 3)),
+            dma((2, 3, 2, 2, 7)),
+            dma((2, 3, 2, 2, 7)),
+            dma((2, 3, 2, 7)),
+            dma((3, 2, 2, 7)),
+            dma((3, 2, 2, 7)),
+            dma((3, 2, 2, 8)),
         ],
         compiler_params=pltpu.CompilerParams(
             collective_id=0, has_side_effects=True, vmem_limit_bytes=60 * 1024 * 1024

time: 106 us -> 106 us (level)
  no operation moved by 1% of the time
where the time goes in v5:
time: 106 us
  Pallas kernels  103 us (97%)
  local copies, waits for them, and re-layouts  2.53 us (2%)
    pallas_call x1, Pallas kernels, body(): pl.pallas_call(step_kernel, out_shape=(jax.ShapeDtypeStruct((4, 2 * chann...  103 us
    unnamed x7, local copies, waits for them, and re-layouts  2.53 us

profile of v5, /device:TPU:1, one launch (start us, length us, event | category | flops | bytes accessed | tf_op | source)
XLA Modules:
  0.0 106.2 jit_solution(8418416115919602130)
XLA Ops:
  0.6 103.0 %shard_map.85 = (f32[4,1024]{1,0:T(4,128)}, f32[4,512]{1,0:T(4,128)}, f32[1,256]{1,0:T(1,128)}) custom-call(bf16[256,512]{1,0:T(8,128)(2,1)} %bitcast.7, s32[4,256]{1,0:T(4,128)} %bitcast.8, s32[4,256]{1,0:T(4,128)} %bitcast.9, bf16[512,1024]{1,0:T(8,128)(2,1)} %w_now_hbm.1, bf16[512,1024]{1,0:T(8,128)(2,1)} %w_delay_hbm.1, bf16[512,512]{1,0:T(8,128)(2,1)} %w_pred_hbm.1), custom_call_target="tpu_custom_call" | custom-call | tf_op jit(solution)/shard_map/pallas_call | solution.py:554
  103.7 0.0 copy-start
  103.7 1.3 %copy.12 = f32[4,1024]{1,0:T(4,128)} copy(f32[4,1024]{1,0:T(4,128)} %get-tuple-element.6) | data formatting | bytes 32768
  105.0 0.0 copy-done
  105.0 0.0 copy-start.1
  105.0 0.6 copy.13
  105.6 0.0 copy-done.1
  105.6 0.6 copy.14
Async XLA Ops:
  103.7 1.3 %copy-start = (f32[4,512]{1,0:T(4,128)S(1)}, f32[4,512]{1,0:T(4,128)}, u32[]{:S(2)}) copy-start(f32[4,512]{1,0:T(4,128)} %get-tuple-element.7) | copy-start | bytes 24580
  105.0 0.6 copy-start.1

commit v6 on v5

--- a/solution.py
+++ b/solution.py
@@ -105,6 +105,15 @@
     d_pre_ref,
     delay_up_ref,
     pred_up_ref,
+    pred_part_ref,
+    pred_core_ref,
+    pred_sum_ref,
+    pred_wide_ref,
+    pred_half_ref,
+    pred_thin_ref,
+    tail_ref,
+    pred_whole_ref,
+    pred_last_ref,
     part_ref,
     core_ref,
     sum_ref,
@@ -112,6 +121,7 @@
     half_ref,
     thin_ref,
     across_ref,
+    final_ref,
     whole_ref,
     weight_sems,
     rows_y_sems,
@@ -120,9 +130,16 @@
     loss_sems,
     loss_core_sems,
     core_sems,
+    pred_wide_sems,
+    pred_thin_sems,
+    tail_sems,
+    pred_first_sems,
+    pred_second_sems,
+    pred_third_sems,
     wide_sems,
     thin_sems,
     across_sems,
+    final_sems,
     first_sems,
     second_sems,
     third_sems,
@@ -309,144 +326,135 @@
         low = (spread - high.astype(F32)).astype(BF16)
         pulled = product(high, mine_ref[...]) + product(low, mine_ref[...])
         d_pred_ref[...] = ((d_pos * goal + pulled) * inv_root).astype(BF16)
-        swap(turn, 0)
-        mine_first = own_part(0)
+        swap_pred(turn)
+        own_pred = pred_part(c)
         d_context = times_transposed(d_pred_ref[...], pred_ref[...])
         tanh_part = tanh_ref[...]
         gate_part = gate_ref[...]
         d_pre_ref[:, :channels] = (d_context * (1.0 - tanh_part * tanh_part) * gate_part).astype(BF16)
         d_pre_ref[:, channels:] = (d_context * tanh_part * gate_part * (1.0 - gate_part)).astype(BF16)
-        swap(turn, 1)
-        swap(turn, 2)
-        start_wide(turn, 0, mine_first)
-        for t in (1, 2):
-            start_wide(turn, t, own_part(t))
-
-    def own_part(t, cc=c):
-        if t == 0:
-            cols = pl.ds(pl.multiple_of(256 * cc, 256), 256)
-            return contract_rows(context_ref[...], d_pred_ref[:, cols])
-        cols = pl.ds(pl.multiple_of(512 * cc + 256 * (t - 1), 256), 256)
+        swap_delay(turn, 0)
+        swap_delay(turn, 1)
+        start_pred(turn, own_pred)
+        for j in range(2):
+            start_wide(turn, j, delay_part(j, c))
+
+    def pred_part(cc):
+        cols = pl.ds(pl.multiple_of(256 * cc, 256), 256)
+        return contract_rows(context_ref[...], d_pred_ref[:, cols])
+
+    def delay_part(j, cc):
+        cols = pl.ds(pl.multiple_of(512 * cc + 256 * j, 256), 256)
         return contract_rows(delayed_ref[...], d_pre_ref[:, cols])
 
     mate = place(y, z, 1 - c)
     swaps = {}
     wide = {}
     thin = {}
-    crossing = {}
-
-    def swap(turn, t):
-        value = own_part(t, 1 - c).astype(BF16).reshape(NY * NZ, 8, 256)
+
+    def swap_pred(turn):
+        pred_part_ref[turn] = pred_part(1 - c).astype(BF16).reshape(NX, 2, NZ, 8, 256)
+        swaps[turn, 2] = send(pred_part_ref.at[turn], pred_core_ref.at[turn], core_sems.at[turn], 2, mate, x)
+
+    def swap_delay(turn, j):
+        part_ref[turn, j] = delay_part(j, 1 - c).astype(BF16).reshape(NY * NZ, 8, 256)
+        swaps[turn, j] = send(part_ref.at[turn, j], core_ref.at[turn, j], core_sems.at[turn], j, mate, x)
+
+    def start_pred(turn, value):
+        swaps[turn, 2].wait()
+        both = value.reshape(NX, 2, NZ, 8, 256) + pred_core_ref[turn].astype(F32)
+        pred_sum_ref[turn] = both.astype(BF16)
+        for k in (2, 1, 3):
+            there = lax.rem(x + k, NX)
+            wide[turn, 2, k] = send(
+                pred_sum_ref.at[turn, there], pred_wide_ref.at[turn, k - 1], pred_wide_sems.at[turn], k - 1, me, there
+            )
+
+    def start_wide(turn, j, value):
+        swaps[turn, j].wait()
+        both = value.reshape(NY * NZ, 8, 256) + core_ref[turn, j].astype(F32)
+        sum_ref[turn, j] = both.astype(BF16).reshape(NY, NZ, 8, 256)
+        for k in FAR_FIRST:
+            if j == 0:
+                there = others_y[k - 1]
+                src, tm = sum_ref.at[turn, j, there], place(there, z, c)
+            else:
+                there = others_z[k - 1]
+                src, tm = sum_ref.at[turn, j, :, there], place(y, there, c)
+            wide[turn, j, k] = send(src, wide_ref.at[turn, j, k - 1], wide_sems.at[turn, j], k - 1, tm, x)
+
+    def settle_pred_wide(turn):
+        total = pred_sum_ref[turn, x].astype(F32)
+        for k in (1, 3, 2):
+            wide[turn, 2, k].wait()
+            total = total + pred_wide_ref[turn, k - 1].astype(F32)
+        pred_half_ref[turn] = total.astype(BF16)
+        for k in FAR_FIRST:
+            there = others_z[k - 1]
+            thin[turn, 2, k] = send(
+                pred_half_ref.at[turn, :, there],
+                pred_thin_ref.at[turn, k - 1],
+                pred_thin_sems.at[turn],
+                k - 1,
+                place(y, there, c),
+                x,
+            )
+
+    tail = {}
+
+    def settle_pred_thin(turn):
+        total = pred_half_ref[turn, :, z].astype(F32)
+        for k in NEAR_FIRST:
+            thin[turn, 2, k].wait()
+            total = total + pred_thin_ref[turn, k - 1].astype(F32)
+        tail_ref[turn, y] = total.astype(BF16)
+        for k in FAR_FIRST:
+            there = others_y[k - 1]
+            spot = tail_ref.at[turn, y]
+            tail[turn, k] = send(spot, spot, tail_sems.at[turn], k - 1, place(there, z, c), x)
+
+    def pred_total(turn):
+        for k in NEAR_FIRST:
+            tail[turn, k].wait()
+        total = tail_ref[turn, 0].astype(F32)
+        for yy in range(1, NY):
+            total = total + tail_ref[turn, yy].astype(F32)
+        return total
+
+    def settle_wide(turn):
         for j in range(2):
-            part_ref[turn, t, j] = value[:, :, 128 * j : 128 * (j + 1)]
-        swaps[turn, t] = send(part_ref.at[turn, t], core_ref.at[turn, t], core_sems.at[turn], t, mate, x)
-
-    def start_wide(turn, t, value):
-        swaps[turn, t].wait()
-        value = value.reshape(NY * NZ, 8, 256)
-        for j in range(2):
-            both = value[:, :, 128 * j : 128 * (j + 1)] + core_ref[turn, t, j].astype(F32)
-            sum_ref[turn, t, j] = both.astype(BF16).reshape(NY, NZ, 8, 128)
-            for k in FAR_FIRST:
-                if j == 0:
-                    there = others_y[k - 1]
-                    src, tm = sum_ref.at[turn, t, j, there], place(there, z, c)
-                else:
-                    there = others_z[k - 1]
-                    src, tm = sum_ref.at[turn, t, j, :, there], place(y, there, c)
-                wide[turn, t, j, k] = send(
-                    src, wide_ref.at[turn, t, j, k - 1], wide_sems.at[turn, t, j], k - 1, tm, x
-                )
-
-    def settle_wide(turn, t):
-        for j in range(2):
-            own = sum_ref[turn, t, j, y] if j == 0 else sum_ref[turn, t, j, :, z]
+            own = sum_ref[turn, j, y] if j == 0 else sum_ref[turn, j, :, z]
             total = own.astype(F32)
             for k in NEAR_FIRST:
-                wide[turn, t, j, k].wait()
-                total = total + wide_ref[turn, t, j, k - 1].astype(F32)
-            half_ref[turn, t, j] = total.astype(BF16)
+                wide[turn, j, k].wait()
+                total = total + wide_ref[turn, j, k - 1].astype(F32)
+            half_ref[turn, j] = total.astype(BF16)
             for k in FAR_FIRST:
                 there = others_z[k - 1] if j == 0 else others_y[k - 1]
                 tm = place(y, there, c) if j == 0 else place(there, z, c)
-                thin[turn, t, j, k] = send(
-                    half_ref.at[turn, t, j, there],
-                    thin_ref.at[turn, t, j, k - 1],
-                    thin_sems.at[turn, t, j],
+                thin[turn, j, k] = send(
+                    half_ref.at[turn, j, there],
+                    thin_ref.at[turn, j, k - 1],
+                    thin_sems.at[turn, j],
                     k - 1,
                     tm,
                     x,
                 )
 
-    def settle_thin(turn, t):
+    def settle_thin(turn, keep_ref):
         for j in range(2):
-            total = half_ref[turn, t, j, z if j == 0 else y].astype(F32)
+            total = half_ref[turn, j, z if j == 0 else y].astype(F32)
             for k in NEAR_FIRST:
-                thin[turn, t, j, k].wait()
-                total = total + thin_ref[turn, t, j, k - 1].astype(F32)
-            across_ref[turn, t, u, :, 128 * j : 128 * (j + 1)] = total
-        if turn == 0:
-            peers = [(c, lax.rem(x + k, NX)) for k in (2, 1, 3)]
-        else:
-            peers = [(uu % 2, uu // 2) for uu in others_u]
-        spot = across_ref.at[turn, t, u]
-        crossing[turn, t] = [
-            send(spot, spot, across_sems.at[turn, t], k, place(y, z, cc), xx) for k, (cc, xx) in enumerate(peers)
-        ]
-
-    def summed(turn, t, cc):
-        finish(crossing[turn, t])
-        crossing[turn, t] = []
-        total = across_ref[turn, t, cc]
-        for xx in range(1, NX):
-            total = total + across_ref[turn, t, 2 * xx + cc]
-        return total
-
-    first = {}
-    second = {}
-    third = {}
-
-    def settle_cross(t):
-        total = summed(0, t, c).astype(BF16)
-        for j in range(2):
-            whole_ref[c, t, j, y, z] = total[:, 128 * j : 128 * (j + 1)]
-        for k in FAR_FIRST:
-            for j in range(2):
-                there = others_z[k - 1] if j == 0 else others_y[k - 1]
-                tm = place(y, there, c) if j == 0 else place(there, z, c)
-                spot = whole_ref.at[c, t, j, y, z]
-                first[t, j, k] = send(spot, spot, first_sems.at[t, j], k - 1, tm, x)
-
-    def stripe(t, j, along):
-        return whole_ref.at[c, t, j, along] if j == 0 else whole_ref.at[c, t, j, :, along]
-
-    def settle_first(t):
-        for j in range(2):
-            for k in NEAR_FIRST:
-                first[t, j, k].wait()
-            for k in FAR_FIRST:
-                there = others_y[k - 1] if j == 0 else others_z[k - 1]
-                tm = place(there, z, c) if j == 0 else place(y, there, c)
-                spot = stripe(t, j, y if j == 0 else z)
-                second[t, j, k] = send(spot, spot, second_sems.at[t, j], k - 1, tm, x)
-
-    def settle_second(t):
-        third[t] = []
-        if t < 2:
-            for k in NEAR_FIRST:
-                for j in range(2):
-                    second[t, j, k].wait()
-            spot = whole_ref.at[c, t]
-            third[t].append(send(spot, spot, third_sems.at[t, 0], 0, mate, x))
-            return
-        for j in range(2):
-            spot = stripe(t, j, y if j == 0 else z)
-            third[t].append(send(spot, spot, third_sems.at[t, j], 0, mate, x))
-        for k in NEAR_FIRST:
-            for j in range(2):
-                second[t, j, k].wait()
-                spot = stripe(t, j, lax.rem((y if j == 0 else z) + 8 - k, 8))
-                third[t].append(send(spot, spot, third_sems.at[t, j], k, mate, x))
+                thin[turn, j, k].wait()
+                total = total + thin_ref[turn, j, k - 1].astype(F32)
+            keep_ref[u, :, 256 * j : 256 * (j + 1)] = total
+
+    def cross(keep_ref, sems, peers):
+        spot = keep_ref.at[u]
+        return [send(spot, spot, sems, k, place(y, z, cc), xx) for k, (cc, xx) in enumerate(peers)]
+
+    def along(j, at, spare):
+        return place(at, z, c) if (j == 0) == spare else place(y, at, c)
 
     loss_going = []
 
@@ -476,49 +484,89 @@
         loss_going[:] = [send(loss_c_ref, loss_c_in_ref, loss_core_sems, 0, place(y, z, 1 - c), x)]
 
     gradient(w_delay_ref, w_pred_ref, 0)
-    settle_wide(0, 0)
-    settle_wide(0, 1)
-    settle_wide(0, 2)
-    settle_thin(0, 0)
-    settle_thin(0, 1)
-    settle_cross(0)
-    settle_thin(0, 2)
-    settle_cross(1)
-    settle_first(0)
-    settle_cross(2)
-    settle_first(1)
-    settle_second(0)
-    settle_first(2)
-    settle_second(1)
-
-    squares = jnp.zeros((8, 128), F32)
-    for t in range(3):
-        if t == 2:
-            settle_second(2)
-        finish(third[t])
-        for cc in range(2):
-            for j in range(2):
-                piece = whole_ref[cc, t, j].astype(F32).reshape(NY * NZ, 8, 128)
-                squares = squares + jnp.sum(piece * piece, axis=0)
+    settle_pred_wide(0)
+    settle_wide(0)
+    settle_pred_thin(0)
+    settle_thin(0, across_ref)
+    crossing = cross(across_ref, across_sems, [(c, lax.rem(x + k, NX)) for k in (2, 1, 3)])
+
+    first = {}
+    second = {}
+    pred_whole_ref[c, x, :, z] = pred_total(0).astype(BF16)
+    for k in FAR_FIRST:
+        spot = pred_whole_ref.at[c, x, :, z]
+        first[2, k] = send(spot, spot, pred_first_sems, k - 1, place(y, others_z[k - 1], c), x)
+    finish(crossing)
+    total = across_ref[c]
+    for xx in range(1, NX):
+        total = total + across_ref[2 * xx + c]
+    for j in range(2):
+        whole_ref[c, j, y, z] = total[:, 256 * j : 256 * (j + 1)].astype(BF16)
+    for k in FAR_FIRST:
+        for j in range(2):
+            there = others_z[k - 1] if j == 0 else others_y[k - 1]
+            spot = whole_ref.at[c, j, y, z]
+            first[j, k] = send(spot, spot, first_sems.at[j], k - 1, along(j, there, False), x)
+    for k in NEAR_FIRST:
+        first[2, k].wait()
+    for k in (2, 1, 3):
+        spot = pred_whole_ref.at[c, x]
+        second[2, k] = send(spot, spot, pred_second_sems, k - 1, me, lax.rem(x + k, NX))
+
+    def stripe(j, at):
+        return whole_ref.at[c, j, at] if j == 0 else whole_ref.at[c, j, :, at]
+
+    for j in range(2):
+        for k in NEAR_FIRST:
+            first[j, k].wait()
+        for k in FAR_FIRST:
+            there = others_y[k - 1] if j == 0 else others_z[k - 1]
+            spot = stripe(j, y if j == 0 else z)
+            second[j, k] = send(spot, spot, second_sems.at[j], k - 1, along(j, there, True), x)
+    third = []
+    for j in range(2):
+        spot = stripe(j, y if j == 0 else z)
+        third.append(send(spot, spot, third_sems.at[j], 0, mate, x))
+    for k in (1, 3, 2):
+        second[2, k].wait()
+    pred_third = send(pred_whole_ref.at[c], pred_whole_ref.at[c], pred_third_sems, 0, mate, x)
+    for k in NEAR_FIRST:
+        for j in range(2):
+            second[j, k].wait()
+            spot = stripe(j, lax.rem((y if j == 0 else z) + 8 - k, 8))
+            third.append(send(spot, spot, third_sems.at[j], k, mate, x))
+
+    pred_third.wait()
+    squares = jnp.zeros((8, 256), F32)
+    for cc in range(2):
+        piece = pred_whole_ref[cc].astype(F32).reshape(NY * NZ, 8, 256)
+        squares = squares + jnp.sum(piece * piece, axis=0)
+    finish(third)
+    for cc in range(2):
+        for j in range(2):
+            piece = whole_ref[cc, j].astype(F32).reshape(NY * NZ, 8, 256)
+            squares = squares + jnp.sum(piece * piece, axis=0)
     norm = jnp.sqrt(jnp.sum(squares))
     step = RHO / (norm + EPS)
-    for t in range(3):
-        for cc in range(2):
-            for j in range(2):
-                piece = whole_ref[cc, t, j].astype(F32).reshape(channels, 128) * step
-                low = 256 * cc + 128 * j if t == 0 else 512 * cc + 256 * (t - 1) + 128 * j
-                old_ref, new_ref = (w_pred_ref, pred_up_ref) if t == 0 else (w_delay_ref, delay_up_ref)
-                new_ref[:, low : low + 128] = (old_ref[:, low : low + 128].astype(F32) + piece).astype(BF16)
+    for cc in range(2):
+        for j in range(2):
+            piece = whole_ref[cc, j].astype(F32).reshape(channels, 256) * step
+            low = 512 * cc + 256 * j
+            delay_up_ref[:, low : low + 256] = (w_delay_ref[:, low : low + 256].astype(F32) + piece).astype(BF16)
+        piece = pred_whole_ref[cc].astype(F32).reshape(channels, 256) * step
+        low = 256 * cc
+        pred_up_ref[:, low : low + 256] = (w_pred_ref[:, low : low + 256].astype(F32) + piece).astype(BF16)
 
     gradient(delay_up_ref, pred_up_ref, 1)
-    settle_wide(1, 0)
-    settle_wide(1, 1)
+    settle_pred_wide(1)
+    settle_wide(1)
+    settle_pred_thin(1)
     loss_to_z()
-    settle_wide(1, 2)
-    settle_thin(1, 0)
-    settle_thin(1, 1)
+    settle_thin(1, final_ref)
     loss_to_core()
-    settle_thin(1, 2)
+    pred_last_ref[...] = pred_total(1)
+    final_ref[u, :, 512:] = pred_last_ref[y & 1]
+    crossing = cross(final_ref, final_sems, [(uu % 2, uu // 2) for uu in others_u])
     finish(loss_going)
     seat = lax.broadcasted_iota(jnp.int32, (128, 128), 0)
     column = lax.broadcasted_iota(jnp.int32, (128, 128), 1)
@@ -534,15 +582,16 @@
     kept = jnp.where(c == 0, back[:2], back[2:4])
     frame_loss_ref[:, :BLOCK] = kept[:1]
     frame_loss_ref[:, BLOCK:] = kept[1:2]
-    for t in range(3):
-        for cc in range(2):
-            total = summed(1, t, cc)
-            kept = jnp.where(c == 0, total[:4], total[4:])
-            if t == 0:
-                grad_pred_ref[:, 256 * cc : 256 * (cc + 1)] = kept
-            else:
-                low = 512 * cc + 256 * (t - 1)
-                grad_delay_ref[:, low : low + 256] = kept
+    finish(crossing)
+    for cc in range(2):
+        total = final_ref[cc, :, :512]
+        for xx in range(1, NX):
+            total = total + final_ref[2 * xx + cc, :, :512]
+        kept = jnp.where(c == 0, total[:4], total[4:])
+        grad_delay_ref[:, 512 * cc : 512 * (cc + 1)] = kept
+        total = final_ref[2 * (y // 2) + cc, :, 512:]
+        kept = jnp.where(c == 0, total[:4], total[4:])
+        grad_pred_ref[:, 256 * cc : 256 * (cc + 1)] = kept
 
 
 def body(latents, w_now, w_delay, w_pred, neg_owner, neg_block):
@@ -593,14 +642,24 @@
             pltpu.VMEM((rows, 2 * channels), BF16),
             pltpu.VMEM((channels, 2 * channels), BF16),
             pltpu.VMEM((channels, channels), BF16),
-            pltpu.VMEM((2, 3, 2, NY * NZ, 8, 128), BF16),
-            pltpu.VMEM((2, 3, 2, NY * NZ, 8, 128), BF16),
-            pltpu.VMEM((2, 3, 2, NY, NZ, 8, 128), BF16),
-            pltpu.VMEM((2, 3, 2, 7, 8, 8, 128), BF16),
-            pltpu.VMEM((2, 3, 2, 8, 8, 128), BF16),
-            pltpu.VMEM((2, 3, 2, 7, 8, 128), BF16),
-            pltpu.VMEM((2, 3, 2 * NX, 8, 256), F32),
-            pltpu.VMEM((2, 3, 2, NY, NZ, 8, 128), BF16),
+            pltpu.VMEM((2, NX, 2, NZ, 8, 256), BF16),
+            pltpu.VMEM((2, NX, 2, NZ, 8, 256), BF16),
+            pltpu.VMEM((2, NX, 2, NZ, 8, 256), BF16),
+            pltpu.VMEM((2, NX - 1, 2, NZ, 8, 256), BF16),
+            pltpu.VMEM((2, 2, NZ, 8, 256), BF16),
+            pltpu.VMEM((2, 7, 2, 8, 256), BF16),
+            pltpu.VMEM((2, NY, 2, 8, 256), BF16),
+            pltpu.VMEM((2, NX, 2, NZ, 8, 256), BF16),
+            pltpu.VMEM((2, 8, 256), F32),
+            pltpu.VMEM((2, 2, NY * NZ, 8, 256), BF16),
+            pltpu.VMEM((2, 2, NY * NZ, 8, 256), BF16),
+            pltpu.VMEM((2, 2, NY, NZ, 8, 256), BF16),
+            pltpu.VMEM((2, 2, 7, 8, 8, 256), BF16),
+            pltpu.VMEM((2, 2, 8, 8, 256), BF16),
+            pltpu.VMEM((2, 2, 7, 8, 256), BF16),
+            pltpu.VMEM((2 * NX, 8, 512), F32),
+            pltpu.VMEM((2 * NX, 8, 768), F32),
+            pltpu.VMEM((2, 2, NY, NZ, 8, 256), BF16),
             dma((6,)),
             dma((2, 2, 7)),
             dma((2, 2, 15)),
@@ -608,12 +667,19 @@
             dma((2, 2, 7)),
             dma((2, 1)),
             dma((2, 2, 3)),
-            dma((2, 3, 2, 2, 7)),
-            dma((2, 3, 2, 2, 7)),
-            dma((2, 3, 2, 7)),
-            dma((3, 2, 2, 7)),
-            dma((3, 2, 2, 7)),
-            dma((3, 2, 2, 8)),
+            dma((2, 2, 3)),
+            dma((2, 2, 7)),
+            dma((2, 2, 7)),
+            dma((2, 7)),
+            dma((2, 3)),
+            dma((2, 1)),
+            dma((2, 2, 2, 7)),
+            dma((2, 2, 2, 7)),
+            dma((2, 3)),
+            dma((2, 7)),
+            dma((2, 2, 7)),
+            dma((2, 2, 7)),
+            dma((2, 2, 8)),
         ],
         compiler_params=pltpu.CompilerParams(
             collective_id=0, has_side_effects=True, vmem_limit_bytes=60 * 1024 * 1024

time: 106 us -> 98.5 us (0.929)
  Pallas kernels: 103 us -> 95.1 us
    pallas_call x1, Pallas kernels: 103 us -> 95.1 us  [body(): pl.pallas_call(step_kernel, out_shape=(jax.ShapeDtypeStruct((4, 2 * chann...]
where the time goes in v6:
time: 98.5 us; the launch traced here: 98.3 us
  Pallas kernels  95.1 us (97%)
  local copies, waits for them, and re-layouts  2.53 us (3%)
    pallas_call x1, Pallas kernels, body(): pl.pallas_call(step_kernel, out_shape=(jax.ShapeDtypeStruct((4, 2 * chann...  95.1 us
    unnamed x7, local copies, waits for them, and re-layouts  2.53 us

profile of v6, /device:TPU:1, one launch (start us, length us, event | category | flops | bytes accessed | tf_op | source)
XLA Modules:
  0.0 98.3 jit_solution(14077763895453246399)
XLA Ops:
  0.6 95.1 %shard_map.85 = (f32[4,1024]{1,0:T(4,128)}, f32[4,512]{1,0:T(4,128)}, f32[1,256]{1,0:T(1,128)}) custom-call(bf16[256,512]{1,0:T(8,128)(2,1)} %bitcast.7, s32[4,256]{1,0:T(4,128)} %bitcast.8, s32[4,256]{1,0:T(4,128)} %bitcast.9, bf16[512,1024]{1,0:T(8,128)(2,1)} %w_now_hbm.1, bf16[512,1024]{1,0:T(8,128)(2,1)} %w_delay_hbm.1, bf16[512,512]{1,0:T(8,128)(2,1)} %w_pred_hbm.1), custom_call_target="tpu_custom_call" | custom-call | tf_op jit(solution)/shard_map/pallas_call | solution.py:603
  95.8 0.0 copy-start
  95.8 1.3 %copy.12 = f32[4,1024]{1,0:T(4,128)} copy(f32[4,1024]{1,0:T(4,128)} %get-tuple-element.6) | data formatting | bytes 32768
  97.1 0.0 copy-done
  97.1 0.0 copy-start.1
  97.1 0.6 copy.13
  97.7 0.0 copy-done.1
  97.8 0.6 copy.14
Async XLA Ops:
  95.8 1.3 %copy-start = (f32[4,512]{1,0:T(4,128)S(1)}, f32[4,512]{1,0:T(4,128)}, u32[]{:S(2)}) copy-start(f32[4,512]{1,0:T(4,128)} %get-tuple-element.7) | copy-start | bytes 24580
  97.1 0.6 copy-start.1

commit v7 on v6

--- a/solution.py
+++ b/solution.py
@@ -296,6 +296,16 @@
         against = [
             jnp.sum(jnp.where(hot[n], pairs, 0.0), axis=1, keepdims=True) * inv_root for n in range(NNEG)
         ]
+        peak = against[0]
+        for score in against[1:]:
+            peak = jnp.maximum(peak, score)
+        lifts = [jnp.exp(score - peak) for score in against]
+        spread = jnp.zeros((rows, rows), F32)
+        for n in range(NNEG):
+            spread = spread + jnp.where(hot[n], lifts[n], 0.0)
+        high = spread.astype(BF16)
+        low = (spread - high.astype(F32)).astype(BF16)
+        pulled = product(high, mine_ref[...]) + product(low, mine_ref[...])
         if turn == 0:
             finish(ahead)
             raw = target_ref[...].astype(F32)
@@ -303,12 +313,8 @@
             target_ref[...] = jnp.where(wraps, moved, raw).astype(BF16)
         goal = target_ref[...].astype(F32)
         positive = jnp.sum(predicted.astype(F32) * goal, axis=1, keepdims=True) * inv_root
-        top = positive
-        for score in against:
-            top = jnp.maximum(top, score)
-        total = jnp.exp(positive - top)
-        for score in against:
-            total = total + jnp.exp(score - top)
+        top = jnp.maximum(peak, positive)
+        total = (lifts[0] + lifts[1] + lifts[2] + lifts[3]) * jnp.exp(peak - top) + jnp.exp(positive - top)
         lse = top + jnp.log(total)
         if turn == 1:
             losses = jnp.broadcast_to(valid * (lse - positive), (rows, 128))
@@ -319,13 +325,8 @@
                 )
         scale = loss_weight * valid
         d_pos = scale * (jnp.exp(positive - lse) - 1.0)
-        spread = jnp.zeros((rows, rows), F32)
-        for n in range(NNEG):
-            spread = spread + jnp.where(hot[n], scale * jnp.exp(against[n] - lse), 0.0)
-        high = spread.astype(BF16)
-        low = (spread - high.astype(F32)).astype(BF16)
-        pulled = product(high, mine_ref[...]) + product(low, mine_ref[...])
-        d_pred_ref[...] = ((d_pos * goal + pulled) * inv_root).astype(BF16)
+        d_neg = scale * jnp.exp(peak - lse)
+        d_pred_ref[...] = ((d_pos * goal + d_neg * pulled) * inv_root).astype(BF16)
         swap_pred(turn)
         own_pred = pred_part(c)
         d_context = times_transposed(d_pred_ref[...], pred_ref[...])
@@ -447,7 +448,7 @@
             for k in NEAR_FIRST:
                 thin[turn, j, k].wait()
                 total = total + thin_ref[turn, j, k - 1].astype(F32)
-            keep_ref[u, :, 256 * j : 256 * (j + 1)] = total
+            keep_ref[u, :, 256 * j : 256 * (j + 1)] = total.astype(BF16)
 
     def cross(keep_ref, sems, peers):
         spot = keep_ref.at[u]
@@ -497,9 +498,9 @@
         spot = pred_whole_ref.at[c, x, :, z]
         first[2, k] = send(spot, spot, pred_first_sems, k - 1, place(y, others_z[k - 1], c), x)
     finish(crossing)
-    total = across_ref[c]
+    total = across_ref[c].astype(F32)
     for xx in range(1, NX):
-        total = total + across_ref[2 * xx + c]
+        total = total + across_ref[2 * xx + c].astype(F32)
     for j in range(2):
         whole_ref[c, j, y, z] = total[:, 256 * j : 256 * (j + 1)].astype(BF16)
     for k in FAR_FIRST:
@@ -536,16 +537,15 @@
             spot = stripe(j, lax.rem((y if j == 0 else z) + 8 - k, 8))
             third.append(send(spot, spot, third_sems.at[j], k, mate, x))
 
+    def squares_of(ref, *at):
+        piece = ref[at].astype(F32).reshape(NY * NZ, 8, 256)
+        return jnp.sum(piece * piece, axis=0)
+
+    own_squares = squares_of(whole_ref, c, 0) + squares_of(whole_ref, c, 1)
     pred_third.wait()
-    squares = jnp.zeros((8, 256), F32)
-    for cc in range(2):
-        piece = pred_whole_ref[cc].astype(F32).reshape(NY * NZ, 8, 256)
-        squares = squares + jnp.sum(piece * piece, axis=0)
+    squares = squares_of(pred_whole_ref, 0) + squares_of(pred_whole_ref, 1)
     finish(third)
-    for cc in range(2):
-        for j in range(2):
-            piece = whole_ref[cc, j].astype(F32).reshape(NY * NZ, 8, 256)
-            squares = squares + jnp.sum(piece * piece, axis=0)
+    squares = squares + (own_squares + (squares_of(whole_ref, 1 - c, 0) + squares_of(whole_ref, 1 - c, 1)))
     norm = jnp.sqrt(jnp.sum(squares))
     step = RHO / (norm + EPS)
     for cc in range(2):
@@ -565,7 +565,7 @@
     settle_thin(1, final_ref)
     loss_to_core()
     pred_last_ref[...] = pred_total(1)
-    final_ref[u, :, 512:] = pred_last_ref[y & 1]
+    final_ref[u, :, 512:] = pred_last_ref[y & 1].astype(BF16)
     crossing = cross(final_ref, final_sems, [(uu % 2, uu // 2) for uu in others_u])
     finish(loss_going)
     seat = lax.broadcasted_iota(jnp.int32, (128, 128), 0)
@@ -584,12 +584,12 @@
     frame_loss_ref[:, BLOCK:] = kept[1:2]
     finish(crossing)
     for cc in range(2):
-        total = final_ref[cc, :, :512]
+        total = final_ref[cc, :, :512].astype(F32)
         for xx in range(1, NX):
-            total = total + final_ref[2 * xx + cc, :, :512]
+            total = total + final_ref[2 * xx + cc, :, :512].astype(F32)
         kept = jnp.where(c == 0, total[:4], total[4:])
         grad_delay_ref[:, 512 * cc : 512 * (cc + 1)] = kept
-        total = final_ref[2 * (y // 2) + cc, :, 512:]
+        total = final_ref[2 * (y // 2) + cc, :, 512:].astype(F32)
         kept = jnp.where(c == 0, total[:4], total[4:])
         grad_pred_ref[:, 256 * cc : 256 * (cc + 1)] = kept
 
@@ -657,8 +657,8 @@
             pltpu.VMEM((2, 2, 7, 8, 8, 256), BF16),
             pltpu.VMEM((2, 2, 8, 8, 256), BF16),
             pltpu.VMEM((2, 2, 7, 8, 256), BF16),
-            pltpu.VMEM((2 * NX, 8, 512), F32),
-            pltpu.VMEM((2 * NX, 8, 768), F32),
+            pltpu.VMEM((2 * NX, 8, 512), BF16),
+            pltpu.VMEM((2 * NX, 8, 768), BF16),
             pltpu.VMEM((2, 2, NY, NZ, 8, 256), BF16),
             dma((6,)),
             dma((2, 2, 7)),
@@ -682,9 +682,21 @@
             dma((2, 2, 8)),
         ],
         compiler_params=pltpu.CompilerParams(
-            collective_id=0, has_side_effects=True, vmem_limit_bytes=60 * 1024 * 1024
+            collective_id=0, has_side_effects=True, vmem_limit_bytes=48 * 1024 * 1024
         ),
-    )(codes, jnp.swapaxes(neg_owner[0], 0, 1), jnp.swapaxes(neg_block[0], 0, 1), w_now, w_delay, w_pred)
+    )(
+        *(
+            pltpu.with_memory_space_constraint(value, pltpu.HBM)
+            for value in (
+                codes,
+                jnp.swapaxes(neg_owner[0], 0, 1),
+                jnp.swapaxes(neg_block[0], 0, 1),
+                w_now,
+                w_delay,
+                w_pred,
+            )
+        )
+    )
 
 
 def solution(mesh):

time: 98.5 us -> 96.2 us (0.977)
  Pallas kernels: 95.1 us -> 93.6 us
    pallas_call x1, Pallas kernels: 95.1 us -> 93.6 us  [body(): pl.pallas_call(step_kernel, out_shape=(jax.ShapeDtypeStruct((4, 2 * chann...]
    unnamed x7 -> x3, local copies, waits for them, and re-layouts: 2.53 us -> 1.77 us
where the time goes in v7:
time: 96.2 us; the launch traced here: 96 us
  Pallas kernels  93.6 us (97%)
  local copies, waits for them, and re-layouts  1.77 us (2%)
    pallas_call x1, Pallas kernels, body(): pl.pallas_call(step_kernel, out_shape=(jax.ShapeDtypeStruct((4, 2 * chann...  93.6 us

profile of v7, /device:TPU:1, one launch (start us, length us, event | category | flops | bytes accessed | tf_op | source)
XLA Modules:
  0.0 96.0 jit_solution(1360035558936010098)
XLA Ops:
  0.6 93.6 %shard_map.85 = (f32[4,1024]{1,0:T(4,128)S(1)}, f32[4,512]{1,0:T(4,128)S(1)}, f32[1,256]{1,0:T(1,128)S(1)}) custom-call(bf16[256,512]{1,0:T(8,128)(2,1)} %bitcast.7, s32[4,256]{1,0:T(4,128)} %bitcast.8, s32[4,256]{1,0:T(4,128)} %bitcast.9, bf16[512,1024]{1,0:T(8,128)(2,1)} %w_now_hbm.1, bf16[512,1024]{1,0:T(8,128)(2,1)} %w_delay_hbm.1, ...), custom_call_target="tpu_custom_call" | custom-call | tf_op jit(solution)/shard_map/pallas_call | solution.py:603
  94.3 0.6 copy.12
  94.9 0.6 copy.13
  95.5 0.6 copy.14

commit v8 on v7

--- a/solution.py
+++ b/solution.py
@@ -253,16 +253,16 @@
 
     going_a = over_y(out_a1_ref, in_a1_ref, 0)
     going_b = over_v(out_b1_ref, in_b1_ref, 0)
+    finish(going_b)
+    out_b2_ref[...] = product(from_vy, in_b1_ref[...].reshape(rows, 256)).astype(BF16).reshape(out_b2_ref.shape)
+    later_b = over_y(out_b2_ref, in_b2_ref, 1)
     finish(going_a)
     out_a2_ref[...] = product(from_yv, in_a1_ref[...].reshape(rows, cut_a)).astype(BF16).reshape(out_a2_ref.shape)
-    going_a = over_v(out_a2_ref, in_a2_ref, 1)
-    finish(going_b)
-    out_b2_ref[...] = product(from_vy, in_b1_ref[...].reshape(rows, 256)).astype(BF16).reshape(out_b2_ref.shape)
-    going_b = over_y(out_b2_ref, in_b2_ref, 1)
-    finish(going_a)
+    later_a = over_v(out_a2_ref, in_a2_ref, 1)
+    finish(later_a)
     mine_ref[:, :cut_a] = product(from_vy, in_a2_ref[...].reshape(rows, cut_a)).astype(BF16)
     ahead = [send(mine_ref.at[:, :cut_a], target_ref.at[:, :cut_a], ring_sems, 0, ring_before, x)]
-    finish(going_b)
+    finish(later_b)
     mine_ref[:, cut_a:] = in_b2_ref[:, :, :128].reshape(rows, 128)
     chosen_ref[...] = in_b2_ref[:, :, 128:].reshape(rows, 128).astype(F32).astype(jnp.int32)
     ahead.append(send(mine_ref.at[:, cut_a:], target_ref.at[:, cut_a:], ring_sems, 1, ring_before, x))
@@ -328,7 +328,6 @@
         d_neg = scale * jnp.exp(peak - lse)
         d_pred_ref[...] = ((d_pos * goal + d_neg * pulled) * inv_root).astype(BF16)
         swap_pred(turn)
-        own_pred = pred_part(c)
         d_context = times_transposed(d_pred_ref[...], pred_ref[...])
         tanh_part = tanh_ref[...]
         gate_part = gate_ref[...]
@@ -336,7 +335,7 @@
         d_pre_ref[:, channels:] = (d_context * tanh_part * gate_part * (1.0 - gate_part)).astype(BF16)
         swap_delay(turn, 0)
         swap_delay(turn, 1)
-        start_pred(turn, own_pred)
+        start_pred(turn, pred_part(c))
         for j in range(2):
             start_wide(turn, j, delay_part(j, c))
 

time: 96.2 us -> 96 us (level)
  no operation moved by 1% of the time
where the time goes in v8:
time: 96 us; the launch traced here: 95.8 us
  Pallas kernels  93.4 us (97%)
  local copies, waits for them, and re-layouts  1.77 us (2%)
    pallas_call x1, Pallas kernels, body(): pl.pallas_call(step_kernel, out_shape=(jax.ShapeDtypeStruct((4, 2 * chann...  93.4 us

profile of v8, /device:TPU:1, one launch (start us, length us, event | category | flops | bytes accessed | tf_op | source)
XLA Modules:
  0.0 95.8 jit_solution(12842408112536471538)
XLA Ops:
  0.6 93.4 %shard_map.85 = (f32[4,1024]{1,0:T(4,128)S(1)}, f32[4,512]{1,0:T(4,128)S(1)}, f32[1,256]{1,0:T(1,128)S(1)}) custom-call(bf16[256,512]{1,0:T(8,128)(2,1)} %bitcast.7, s32[4,256]{1,0:T(4,128)} %bitcast.8, s32[4,256]{1,0:T(4,128)} %bitcast.9, bf16[512,1024]{1,0:T(8,128)(2,1)} %w_now_hbm.1, bf16[512,1024]{1,0:T(8,128)(2,1)} %w_delay_hbm.1, ...), custom_call_target="tpu_custom_call" | custom-call | tf_op jit(solution)/shard_map/pallas_call | solution.py:602
  94.1 0.6 copy.12
  94.7 0.6 copy.13
  95.3 0.6 copy.14
